TPU v7x, 32 devices: a whole 2x2x4 slice. The times are simulated.
32 devices in a mesh: row: 8 (over z, x), col: 2 (over y), snode: 2 (over core).
Axes of the slice: x: 2, y: 2, z: 4, core: 2. Of those that a mesh axis runs over, the one named last changes fastest.
Arguments:
- ancestor_inverse: bfloat16 [40960, 20480], P(('snode', 'row'), 'col'), parts along dimension 0, may hold values from -8 to 8
- fill_mask: int32 [160, 80], P('snode'), parts along dimension 0, may hold values from 0 to 1, as said below
- block_order: int32 [4, 80], P('snode'), parts along dimension 0, may hold values from 0 to 79, each once within a row
- l_rows: bfloat16 [4, 20480, 256], P('snode', ('row', 'col')), parts along dimension 0, may hold values from -6 to 6
- diag_inverse: bfloat16 [4, 256, 256], P('snode'), parts along dimension 0, may hold values from -0.0024414062 to 0.0024414062
Outputs:
- ainv_kr: bfloat16 [4, 256, 20480], P('snode', None, ('row', 'col')), parts along dimension 0
There are 2 independent parts, one for each index of `snode`. A program takes and returns all parts, laid end to end along the dimension named above; each array names one. Nothing has to cross between parts.
Inputs may be any that keep to these rules, and one draw needn't show every extreme that they name: Tile (i, j) takes part exactly where fill_mask is 1; diagonal tiles are always 1. `block_order`: each row is a permutation of the 80 ancestor blocks.
All inputs are finite; a program needn't handle non-finite values.
Results may differ from a plain program's by a relative error of at most 0.014.
Values may be sent and summed in bfloat16 or wider, within the bound.
A program may use at most 256 MiB of HBM per device.

v0:
```python
import functools

import jax
import jax.numpy as jnp
from jax import lax
from jax.experimental import pallas as pl
from jax.experimental.pallas import tpu as pltpu
from jax.sharding import PartitionSpec as P

MESH = pl.DeviceIdType.MESH
UP, DOWN, XP, YP = range(4)


def gather_plan(blocks):
    fifth = blocks // 5
    half = max(fifth, 1)
    plan = []
    start = 0
    for order, share in (("zxy", 2 * fifth), ("zyx", 2 * fifth), ("xyz", fifth // 2)):
        while share > 0:
            size = min(half, share)
            plan.append((start, size, order))
            start += size
            share -= size
    while start < blocks:
        size = min(half, blocks - start)
        size = min(size, max(fifth // 2, 1))
        plan.append((start, size, "yxz"))
        start += size
    rank = {"zxy": 0, "zyx": 1, "xyz": 2, "yxz": 3}
    count = {}
    keyed = []
    for piece in plan:
        n = count.get(piece[2], 0)
        count[piece[2]] = n + 1
        keyed.append((n, rank[piece[2]], piece))
    return [piece for _, _, piece in sorted(keyed)]


def gather_kernel(depth, plan, own_ref, out_ref, send_sem, recv_sem, local_sem):
    row = lax.axis_index("row")
    y = lax.axis_index("col")
    core = lax.axis_index("snode")
    z = row // 2
    x = row % 2
    where = {
        UP: ((z + 1) * 2 + x, y, core),
        DOWN: ((z - 1) * 2 + x, y, core),
        XP: (z * 2 + 1 - x, y, core),
        YP: (row, 1 - y, core),
    }
    exists = {UP: z + 1 < depth, DOWN: z >= 1}

    barrier = pltpu.get_barrier_semaphore()
    for way in (XP, YP):
        pl.semaphore_signal(barrier, inc=1, device_id=where[way], device_id_type=MESH)
    for way in (UP, DOWN):

        @pl.when(exists[way])
        def _():
            pl.semaphore_signal(barrier, inc=1, device_id=where[way], device_id_type=MESH)

    ends = (depth > 1) + (depth > 2)
    inner = jnp.logical_and(exists[UP], exists[DOWN])

    @pl.when(inner)
    def _():
        pl.semaphore_wait(barrier, 2 + ends)

    @pl.when(jnp.logical_not(inner))
    def _():
        pl.semaphore_wait(barrier, 2 + (depth > 1))

    me = row * 2 + y

    def slot_of(zz, xx, yy):
        return (zz * 2 + xx) * 2 + yy

    sent = []

    def descriptor(number, slot, own, way, target=None):
        start, size, _ = plan[number]
        span = pl.ds(start, size)
        source = own_ref.at[span] if own else out_ref.at[slot, span]
        return pltpu.make_async_remote_copy(
            src_ref=source,
            dst_ref=out_ref.at[slot, span],
            send_sem=send_sem.at[way, slot, number],
            recv_sem=recv_sem.at[slot, number],
            device_id=where[way] if target is None else target,
            device_id_type=MESH,
        )

    def guarded(cond, fn):
        if cond is None:
            fn()
        else:
            pl.when(cond)(fn)

    def both(a, b):
        if a is None:
            return b
        if b is None:
            return a
        return jnp.logical_and(a, b)

    def send(number, slot, own, way, cond):
        cond = both(cond, exists.get(way))
        guarded(cond, lambda: descriptor(number, slot, own, way).start())
        sent.append((number, slot, own, way, cond))

    def arrived(number, slot, cond):
        guarded(cond, lambda: descriptor(number, slot, False, XP).wait_recv())

    local = pltpu.make_async_copy(own_ref, out_ref.at[me], local_sem)
    local.start()

    partner = {"x": XP, "y": YP}

    def coords(flip_x, flip_y):
        return (1 - x if flip_x else x), (1 - y if flip_y else y)

    reach = [0]
    for k in range(1, depth):
        reach += [-k, k]

    def near(dz):
        if dz == 0:
            return None
        return z + dz >= 0 if dz < 0 else z + dz < depth

    def onward_z(number, slot, own, dz, cond):
        if dz <= 0:
            send(number, slot, own, UP, cond)
        if dz >= 0:
            send(number, slot, own, DOWN, cond)

    def z_first(number, order, dz, level):
        first, second = order[1], order[2]
        flips = {0: "", 1: first, 2: second, 3: "xy"}[level]
        xx, yy = coords("x" in flips, "y" in flips)
        slot = slot_of(z + dz, xx, yy)
        own = level == 0 and dz == 0
        cond = near(dz)
        if not own:
            arrived(number, slot, cond)
        if level == 0:
            onward_z(number, slot, own, dz, cond)
            send(number, slot, own, partner[first], cond)
            send(number, slot, own, partner[second], cond)
        elif level == 1:
            send(number, slot, own, partner[second], cond)

    def z_last(number, order, dz, level):
        first, second = order[0], order[1]
        flips = {0: "", 1: first, 2: second, 3: "xy"}[level]
        xx, yy = coords("x" in flips, "y" in flips)
        slot = slot_of(z + dz, xx, yy)
        own = level == 0 and dz == 0
        cond = near(dz)
        if not own:
            arrived(number, slot, cond)
        onward_z(number, slot, own, dz, cond)
        if dz == 0:
            if level == 0:
                send(number, slot, own, partner[first], cond)
            if level in (0, 1):
                send(number, slot, own, partner[second], cond)

    def handle(number, dz, level):
        order = plan[number][2]
        (z_first if order[0] == "z" else z_last)(number, order, dz, level)

    numbers = range(len(plan))
    events = []
    for number in numbers:
        for position, dz in enumerate(reach):
            hop = (position + 1) // 2
            for level in range(4):
                events.append((2 * hop + (0, 2, 2, 4)[level], number, position, level, dz))
    events.sort(key=lambda e: e[:4])
    for _, number, _, level, dz in events:
        handle(number, dz, level)
    for number, slot, own, way, cond in sent:
        guarded(cond, lambda: descriptor(number, slot, own, way).wait_send())
    local.wait()


def gather(own, row_size, col_size):
    depth = row_size // 2
    blocks = own.shape[0]
    plan = gather_plan(blocks)
    devices = row_size * col_size
    return pl.pallas_call(
        functools.partial(gather_kernel, depth, plan),
        out_shape=jax.ShapeDtypeStruct((devices,) + own.shape, own.dtype),
        in_specs=[pl.BlockSpec(memory_space=pl.ANY)],
        out_specs=pl.BlockSpec(memory_space=pl.ANY),
        scratch_shapes=[
            pltpu.SemaphoreType.DMA((4, devices, len(plan))),
            pltpu.SemaphoreType.DMA((devices, len(plan))),
            pltpu.SemaphoreType.DMA,
        ],
        compiler_params=pltpu.CompilerParams(collective_id=0, has_side_effects=True),
        name="gather",
    )(own)


def product_kernel(snodes, width, tile, table_ref, gate_ref, half_ref, a_ref, *rest):
    piece_refs = rest[: snodes * width]
    out_ref, stack_ref, total_ref = rest[snodes * width :]
    step = pl.program_id(0)
    for b in range(width):
        for s in range(snodes):
            stack_ref[b * tile : (b + 1) * tile, s * tile : (s + 1) * tile] = piece_refs[
                b * snodes + s
            ][...]

    @pl.when(step == 0)
    def _():
        total_ref[...] = jnp.zeros_like(total_ref)

    row_tiles = a_ref.shape[0] // tile
    for i in range(row_tiles):
        rows = slice(i * tile, (i + 1) * tile)
        parts = []
        for b in range(width):
            gate = gate_ref[half_ref[0] * row_tiles + i, step * width + b]
            part = a_ref[rows, b * tile : (b + 1) * tile]
            parts.append(part * gate.astype(jnp.float32).astype(part.dtype))
        total_ref[rows, :] += jnp.dot(
            jnp.concatenate(parts, axis=1), stack_ref[...], preferred_element_type=jnp.float32
        )

    @pl.when(step == pl.num_programs(0) - 1)
    def _():
        for i in range(row_tiles):
            rows = slice(i * tile, (i + 1) * tile)
            out_ref[:, rows] = (-total_ref[rows, :]).T.astype(out_ref.dtype)


def product(table, gate, half, ancestor_inverse, pieces, shares, snodes, tile, dtype):
    local_rows, local_cols = ancestor_inverse.shape
    rows = local_rows // shares
    col_blocks = local_cols // tile
    width = max(w for w in range(1, 6) if col_blocks % w == 0)

    def piece_spec(b, s):
        return pl.BlockSpec(
            (pl.Squeezed(), tile, tile),
            lambda k, table_ref, gate_ref, half_ref: (table_ref[s, k * width + b], 0, 0),
        )

    return pl.pallas_call(
        functools.partial(product_kernel, snodes, width, tile),
        out_shape=jax.ShapeDtypeStruct((snodes * tile, rows), dtype),
        grid_spec=pltpu.PrefetchScalarGridSpec(
            num_scalar_prefetch=3,
            grid=(col_blocks // width,),
            in_specs=[
                pl.BlockSpec((rows, width * tile), lambda k, t, g, half_ref: (half_ref[0], k))
            ]
            + [piece_spec(b, s) for b in range(width) for s in range(snodes)],
            out_specs=pl.BlockSpec((snodes * tile, rows), lambda k, t, g, h: (0, 0)),
            scratch_shapes=[
                pltpu.VMEM((width * tile, snodes * tile), jnp.bfloat16),
                pltpu.VMEM((rows, snodes * tile), jnp.float32),
            ],
        ),
        compiler_params=pltpu.CompilerParams(
            dimension_semantics=("arbitrary",), vmem_limit_bytes=56 * 1024 * 1024
        ),
        cost_estimate=pl.CostEstimate(
            flops=2 * rows * local_cols * snodes * tile,
            bytes_accessed=2 * rows * local_cols,
            transcendentals=0,
        ),
        name="product",
    )(table, gate, half, ancestor_inverse, *([pieces] * (snodes * width)))


def fast(ancestor_inverse, fill_mask, block_order, l_rows, diag_inverse):
    row_index = lax.axis_index("row")
    col_index = lax.axis_index("col")
    row_size = lax.axis_size("row")
    col_size = lax.axis_size("col")
    local_rows, local_cols = ancestor_inverse.shape
    snodes, tile = diag_inverse.shape[:2]
    row_blocks = local_rows // tile
    col_blocks = local_cols // tile
    held = l_rows.shape[1] // tile
    normed = jnp.einsum(
        "sxy,syz->sxz", l_rows, diag_inverse, preferred_element_type=jnp.float32
    ).astype(jnp.bfloat16)
    own = normed.reshape(snodes * held, tile, tile)
    pieces = gather(own, row_size, col_size).reshape(-1, tile, tile)

    wanted = col_index * col_blocks + jnp.arange(col_blocks, dtype=jnp.int32)
    packed = jnp.arange(block_order.shape[1], dtype=jnp.int32)
    place = jnp.sum(
        jnp.where(block_order[:, None, :] == wanted[None, :, None], packed[None, None, :], 0), axis=2
    )
    table = (
        (place // held) * (snodes * held)
        + jnp.arange(snodes, dtype=jnp.int32)[:, None] * held
        + place % held
    ).astype(jnp.int32)
    gate = lax.dynamic_slice(
        fill_mask, (row_index * row_blocks, col_index * col_blocks), (row_blocks, col_blocks)
    )

    def share(half, dtype):
        return product(
            table, gate, half.reshape(1).astype(jnp.int32), ancestor_inverse, pieces,
            col_size, snodes, tile, dtype,
        )

    theirs = share(1 - col_index, jnp.bfloat16)
    received = lax.ppermute(theirs, "col", [(0, 1), (1, 0)])
    mine = share(col_index, jnp.float32)
    total = (mine + received.astype(jnp.float32)).astype(jnp.bfloat16)
    return total.reshape(snodes, tile, local_rows // col_size)


def plain(ancestor_inverse, fill_mask, block_order, l_rows, diag_inverse):
    row_index = lax.axis_index("row")
    col_index = lax.axis_index("col")
    local_rows, local_cols = ancestor_inverse.shape
    snode_count, tile_size = diag_inverse.shape[:2]
    block_count = fill_mask.shape[0]
    row_blocks = local_rows // tile_size
    col_blocks = local_cols // tile_size
    normed = jnp.einsum(
        "sxy,syz->sxz", l_rows, diag_inverse, preferred_element_type=jnp.float32
    ).astype(jnp.bfloat16)
    wanted = col_index * col_blocks + jnp.arange(col_blocks, dtype=jnp.int32)
    everything = lax.all_gather(normed, ("row", "col"), axis=1, tiled=True)
    pieces = everything.reshape(snode_count, block_count, tile_size, tile_size)
    selector = (block_order[:, None, :] == wanted[None, :, None]).astype(jnp.bfloat16)
    columns = jnp.einsum(
        "saq,sqxy->saxy", selector, pieces, preferred_element_type=jnp.float32
    ).astype(jnp.bfloat16)
    stacked = columns.transpose(1, 2, 0, 3).reshape(local_cols, snode_count * tile_size)
    tile_gate = lax.dynamic_slice(
        fill_mask, (row_index * row_blocks, col_index * col_blocks), (row_blocks, col_blocks)
    ).astype(jnp.bfloat16)
    masked = (
        ancestor_inverse.reshape(row_blocks, tile_size, col_blocks, tile_size)
        * tile_gate[:, None, :, None]
    ).reshape(local_rows, local_cols)
    share_rows = local_rows // lax.axis_size("col")
    own_rows = lax.psum_scatter(
        (-jnp.dot(masked, stacked, preferred_element_type=jnp.float32)).astype(jnp.bfloat16),
        "col",
        scatter_dimension=0,
        tiled=True,
    ).astype(jnp.float32)
    return (
        own_rows.reshape(share_rows, snode_count, tile_size).transpose(1, 2, 0).astype(jnp.bfloat16)
    )


def per_device(ancestor_inverse, fill_mask, block_order, l_rows, diag_inverse):
    tile = diag_inverse.shape[1]
    col_size = lax.axis_size("col")
    if (
        col_size == 2
        and lax.axis_size("row") % 2 == 0
        and l_rows.shape[1] % tile == 0
        and ancestor_inverse.shape[0] % (col_size * tile) == 0
    ):
        return fast(ancestor_inverse, fill_mask, block_order, l_rows, diag_inverse)
    return plain(ancestor_inverse, fill_mask, block_order, l_rows, diag_inverse)


def solution(mesh):
    return jax.shard_map(
        per_device,
        mesh=mesh,
        in_specs=(
            P(("snode", "row"), "col"),
            P("snode", None),
            P("snode", None),
            P("snode", ("row", "col"), None),
            P("snode", None, None),
        ),
        out_specs=P("snode", None, ("row", "col")),
        check_vma=False,
    )
```

profile of v0, /device:TPU:0, one launch (start us, length us, event | category | flops | bytes accessed | tf_op | source)
XLA Modules:
  0.0 214.5 jit_solution(4937137395382960231)
XLA Ops:
  0.0 0.0 copy-start
  0.0 1.3 copy-done
  1.3 2.5 %convolution_convert_fusion = bf16[2,1280,256]{2,1,0:T(8,128)(2,1)} fusion(bf16[2,1280,256]{2,1,0:T(8,128)(2,1)S(1)} %copy-done, bf16[2,256,256]{2,1,0:T(8,128)(2,1)} %param.9), kind=kOutput, calls=%fused_computation | convolution fusion | flops 336199680 | bytes 2883584 | tf_op jit(solution)/shard_map/sxy,syz->sxz/dot_general | solution.py:292
  3.8 0.0 copy-start.2
  3.8 154.9 %gather.1 = bf16[16,10,256,256]{3,2,1,0:T(8,128)(2,1)} custom-call(bf16[10,256,256]{2,1,0:T(8,128)(2,1)} %bitcast.27), custom_call_target="tpu_custom_call" | custom-call | tf_op jit(solution)/shard_map/gather/pallas_call | solution.py:194
  158.7 0.0 copy-done.2
  158.7 0.2 select_reduce_fusion
  158.9 0.6 fusion.table_ref
  159.6 1.4 dynamic_slice.3.gate_ref
  160.9 22.2 %product.3 = bf16[512,1280]{1,0:T(8,128)(2,1)} custom-call(s32[2,40]{1,0:T(2,128)} %fusion.table_ref, s32[10,40]{1,0:T(8,128)} %dynamic_slice.3.gate_ref, s32[1]{0:T(128)} %bitcast.3.half_ref, bf16[2560,10240]{1,0:T(8,128)(2,1)} %a_ref.3, bf16[160,256,256]{2,1,0:T(8,128)(2,1)} %bitcast.7, bf16[160,256,256]{2,1,0:T(8,128)(2,1)} %bitcast.8, ...), custom_call_target="tpu_custom_call" | custom-call | flops 13421772800 | bytes 26214400 | tf_op jit(solution)/shard_map/product/pallas_call | solution.py:254
  183.1 1.4 collective-permute-start
  184.5 23.0 %product.2 = f32[512,1280]{1,0:T(8,128)} custom-call(s32[2,40]{1,0:T(2,128)} %fusion.table_ref, s32[10,40]{1,0:T(8,128)} %dynamic_slice.3.gate_ref, s32[1]{0:T(128)} %bitcast.half_ref, bf16[2560,10240]{1,0:T(8,128)(2,1)} %a_ref.3, bf16[160,256,256]{2,1,0:T(8,128)(2,1)} %bitcast.17, bf16[160,256,256]{2,1,0:T(8,128)(2,1)} %bitcast.18, ...), custom_call_target="tpu_custom_call" | custom-call | flops 13421772800 | bytes 26214400 | tf_op jit(solution)/shard_map/product/pallas_call | solution.py:254
  207.5 3.8 %collective-permute-done = bf16[512,1280]{1,0:T(8,128)(2,1)S(1)} collective-permute-done((bf16[512,1280]{1,0:T(8,128)(2,1)}, bf16[512,1280]{1,0:T(8,128)(2,1)S(1)}, u32[]{:S(2)}, u32[]{:S(2)}) %collective-permute-start) | collective-permute-done | bytes 1310752 | tf_op jit(solution)/shard_map/ppermute | solution.py:319
  211.3 0.0 copy-start.1
  211.3 3.2 %add_convert_fusion = bf16[512,1280]{1,0:T(8,128)(2,1)} fusion(f32[512,1280]{1,0:T(8,128)} %product.2, bf16[512,1280]{1,0:T(8,128)(2,1)S(1)} %collective-permute-done), kind=kLoop, calls=%fused_computation.1 | loop fusion | flops 1966080 | bytes 5242880 | tf_op jit(solution)/shard_map/convert_element_type | solution.py:321
  214.5 0.0 copy-done.1
  (2 shorter events, 0.0 us)
Async XLA Ops:
  0.0 1.3 copy-start
  3.8 154.9 %copy-start.2 = (s32[2,80]{1,0:T(2,128)S(1)}, s32[2,80]{1,0:T(2,128)}, u32[]{:S(2)}) copy-start(s32[2,80]{1,0:T(2,128)} %param.7) | copy-start | bytes 1924
  183.1 28.2 %collective-permute-start = (bf16[512,1280]{1,0:T(8,128)(2,1)}, bf16[512,1280]{1,0:T(8,128)(2,1)S(1)}, u32[]{:S(2)}, u32[]{:S(2)}) collective-permute-start(bf16[512,1280]{1,0:T(8,128)(2,1)} %product.3), channel_id=1, source_target_pairs={{0,2},{2,0},{1,3},{3,1},{4,6},{6,4},{5,7},{7,5},{8,10},{10,8},{9,1... | collective-permute-start | bytes 3932168 | tf_op jit(solution)/shard_map/ppermute | solution.py:319
  211.3 3.2 %copy-start.1 = (bf16[2,1280,256]{2,1,0:T(8,128)(2,1)S(1)}, bf16[2,1280,256]{2,1,0:T(8,128)(2,1)}, u32[]{:S(2)}) copy-start(bf16[2,1280,256]{2,1,0:T(8,128)(2,1)} %param.8) | copy-start | bytes 3932164
where the time goes:
time: 215 us; the launch traced here: 214 us
  Pallas kernels  200 us (93%)
  other arithmetic  3.98 us (2%)
  waiting for transfers between devices  3.79 us (2%)
  local copies, waits for them, and re-layouts  2.69 us (1%)
  matrix products  2.5 us (1%)
    pallas_call x1, Pallas kernels, gather(): pl.pallas_call(functools.partial(gather_kernel, depth, plan), out_shape=j...  155 us
    pallas_call x2, Pallas kernels, product(): pl.pallas_call(functools.partial(product_kernel, snodes, width, tile), ou...  45.2 us
  transfers between devices with their start and end apart: 1, of which 1 were waited for; matrix products, arithmetic and copies ran while one was open for 0% of the time, Pallas kernels for 11%

commit v1 on v0

v1 whole, which is shorter than its diff:
```python
import functools

import jax
import jax.numpy as jnp
from jax import lax
from jax.experimental import pallas as pl
from jax.experimental.pallas import tpu as pltpu
from jax.sharding import PartitionSpec as P

MESH = pl.DeviceIdType.MESH
LANES = 128
PARTS = 4


def sizes(row_size, snodes, tile, held, local_rows, local_cols):
    depth = row_size // 2
    halves = tile // LANES
    phases = snodes * halves
    blocks = local_cols // tile
    away = [blocks // 4] * phases
    away[0] = 0
    away[-1] = blocks // 10
    return dict(
        depth=depth,
        halves=halves,
        phases=phases,
        snodes=snodes,
        tile=tile,
        held=held,
        blocks=blocks,
        shares=local_rows // (2 * tile),
        away=away,
    )


def fused_kernel(
    cfg, inv_ref, mask_ref, a_ref, l_ref, d_ref, out_ref, *rest
):
    depth, halves, phases = cfg["depth"], cfg["halves"], cfg["phases"]
    snodes, tile, held = cfg["snodes"], cfg["tile"], cfg["held"]
    blocks, shares, away = cfg["blocks"], cfg["shares"], cfg["away"]
    lanes = rest[:phases]
    (
        theirs_ref,
        mine_ref,
        l_vm,
        d_vm,
        own_ref,
        pick_ref,
        cols_ref,
        give_ref,
        take_ref,
        res_ref,
        b_send,
        b_recv,
        c_send,
        c_recv,
        y_send,
        y_recv,
        x_send,
        x_recv,
        f_send,
        f_recv,
        o_send,
        o_recv,
        a_sem,
        m_sem,
        in_sem,
        out_sem,
    ) = rest[phases:]
    quarter = tile // PARTS
    plane = PARTS * held

    row = lax.axis_index("row")
    y = lax.axis_index("col")
    core = lax.axis_index("snode")
    z = row // 2
    x = row % 2
    me = x * 2 + y
    lane_x = (1 - x) * 2 + y
    lane_y = x * 2 + 1 - y
    lane_d = (1 - x) * 2 + 1 - y
    slot = (row * 2 + y) * held

    def at(zz, xx, yy):
        return (zz * 2 + xx, yy, core)

    sides = [(at(z, 1 - x, y), lane_x), (at(z, x, 1 - y), lane_y), (at(z, 1 - x, 1 - y), lane_d)]
    to_x, to_y = sides[0][0], sides[1][0]
    pair = at(z + 1 - 2 * (z % 2), x, y)
    reach = [dz for dz in (2, -2, 1, -1) if abs(dz) < depth]

    def exists(dz):
        return z + dz < depth if dz > 0 else z + dz >= 0

    inner = jnp.logical_and(z >= 1, z + 1 < depth)
    low = z * 2 < depth
    far = jnp.where(low, z + 2, z - 2)
    near = jnp.where(low, z - 1, z + 1)

    loads = []
    for s in range(snodes):
        loads.append(pltpu.make_async_copy(l_ref.at[s], l_vm.at[s], in_sem.at[s, 0]))
        loads.append(pltpu.make_async_copy(d_ref.at[s], d_vm.at[s], in_sem.at[s, 1]))
    for c in loads:
        c.start()

    def theirs_load(i):
        return pltpu.make_async_copy(
            a_ref.at[pl.ds(((1 - y) * shares + i) * tile, tile)],
            theirs_ref.at[pl.ds(i * tile, tile)],
            a_sem.at[i],
        )

    def mine_load(g):
        return pltpu.make_async_copy(
            a_ref.at[pl.ds((y * shares + g % shares) * tile, tile)],
            mine_ref.at[g % 2],
            m_sem.at[g % 2],
        )

    for i in range(shares):
        theirs_load(i).start()
    for g in range(2):
        mine_load(g).start()

    barrier = pltpu.get_barrier_semaphore()
    for dev, _ in sides:
        pl.semaphore_signal(barrier, inc=1, device_id=dev, device_id_type=MESH)
    for dz in reach:

        @pl.when(exists(dz))
        def _():
            pl.semaphore_signal(barrier, inc=1, device_id=at(z + dz, x, y), device_id_type=MESH)

    def normalize(p):
        s, h = p // halves, p % halves
        rows = jnp.dot(
            l_vm[s], d_vm[s, :, h * LANES : (h + 1) * LANES], preferred_element_type=jnp.float32
        ).astype(own_ref.dtype)
        own_ref[p] = rows.reshape(held, PARTS, quarter, LANES).transpose(1, 0, 2, 3)
        lanes[p][pl.ds(slot, held)] = own_ref[p, me]

    for c in loads[:2]:
        c.wait()
    normalize(0)

    @pl.when(inner)
    def _():
        pl.semaphore_wait(barrier, len(sides) + 3)

    @pl.when(jnp.logical_not(inner))
    def _():
        pl.semaphore_wait(barrier, len(sides) + min(2, depth - 1))

    pending = []

    def remote(src, dst, send, recv, dev):
        return pltpu.make_async_remote_copy(
            src_ref=src, dst_ref=dst, send_sem=send, recv_sem=recv, device_id=dev, device_id_type=MESH
        )

    def guarded(cond, fn):
        if cond is None:
            fn()
        else:
            pl.when(cond)(fn)

    def start(make, cond=None):
        guarded(cond, lambda: make().start())
        pending.append((make, cond))

    def b_copy(p, k):
        dev, lane = sides[k]
        return remote(
            own_ref.at[p, lane], lanes[p].at[pl.ds(slot, held)], b_send.at[p, k], b_recv.at[p, k], dev
        )

    def spread(p):
        for k in (2, 0, 1):
            start(lambda k=k: b_copy(p, k))

    def c_copy(p, source, target, index):
        span = pl.ds(source * plane, plane)
        return remote(
            lanes[p].at[span],
            lanes[p].at[span],
            c_send.at[p, index],
            c_recv.at[p, source],
            at(target, x, y),
        )

    def climb(p):
        for k in range(3):
            b_copy(p, k).wait_recv()
        for n, dz in enumerate(reach):
            start(lambda n=n, dz=dz: c_copy(p, z, z + dz, n), exists(dz))

    def relay(p):
        if depth < 4:
            return

        @pl.when(inner)
        def _():
            c_copy(p, far, near, len(reach)).wait_recv()

        start(lambda: c_copy(p, far, near, len(reach)), inner)

    def climbed(p):
        for k in range(1, depth):
            source = (z + k) % depth
            cond = None
            if depth >= 4:
                cond = jnp.logical_not(jnp.logical_and(inner, source == far))
            guarded(cond, lambda: c_copy(p, source, z, 0).wait_recv())

    def y_copy(p):
        return remote(pick_ref.at[p], cols_ref.at[p, me], y_send.at[p], y_recv.at[p], to_y)

    def x_copy(p, k):
        lane = (me, lane_y)[k]
        span = pl.ds((z % 2) * away[p], blocks - away[p])
        return remote(
            cols_ref.at[p, lane, span],
            cols_ref.at[p, lane, span],
            x_send.at[p, k],
            x_recv.at[p, k],
            to_x,
        )

    def f_copy(p, k):
        lane = (lane_x, lane_d)[k]
        span = pl.ds((z % 2) * (blocks - away[p]), away[p])
        return remote(
            cols_ref.at[p, lane, span],
            cols_ref.at[p, lane, span],
            f_send.at[p, k],
            f_recv.at[p, k],
            pair,
        )

    def sort(p):
        climbed(p)
        s = p // halves

        def pick(j, carry):
            pick_ref[p, j] = lanes[p][inv_ref[s, (1 - y) * blocks + j]]
            cols_ref[p, me, j] = lanes[p][inv_ref[s, y * blocks + j]]
            return carry

        lax.fori_loop(0, blocks, pick, 0)
        start(lambda: y_copy(p))
        start(lambda: x_copy(p, 0))

    def pass_on(p):
        y_copy(p).wait_recv()
        start(lambda: x_copy(p, 1))

    def crossed(p):
        for k in range(2):
            x_copy(p, k).wait_recv()
            if away[p]:
                start(lambda k=k: f_copy(p, k))

    def forwarded(p):
        if away[p]:
            for k in range(2):
                f_copy(p, k).wait_recv()

    def gate_of(i, j):
        return mask_ref[i, y * blocks + j].astype(jnp.float32).astype(theirs_ref.dtype)

    def gate_theirs():
        first = row * 2 * shares + (1 - y) * shares

        def one_row(i, carry):
            pltpu.make_async_copy(
                a_ref.at[pl.ds(0, tile)], theirs_ref.at[pl.ds(i * tile, tile)], a_sem.at[i]
            ).wait()
            rows = pl.ds(pl.multiple_of(i * tile, tile), tile)

            def one(j, carry):
                span = pl.ds(pl.multiple_of(j * tile, tile), tile)
                theirs_ref[rows, span] = theirs_ref[rows, span] * gate_of(first + i, j)
                return carry

            return lax.fori_loop(0, blocks, one, carry)

        lax.fori_loop(0, shares, one_row, 0)

    step = max(n for n in range(1, 5) if blocks % n == 0)

    def columns(p, c):
        part = cols_ref[p, :, c * step : (c + 1) * step]
        return part.transpose(1, 0, 2, 3).reshape(step * tile, LANES)

    def o_copy(p, i):
        return remote(give_ref.at[p, i], take_ref.at[p, i], o_send.at[p, i], o_recv.at[p, i], to_y)

    def theirs(p):
        def block(i, carry):
            rows = pl.ds(pl.multiple_of(i * tile, tile), tile)
            total = jnp.zeros((tile, LANES), jnp.float32)
            for c in range(blocks // step):
                total += jnp.dot(
                    theirs_ref[rows, c * step * tile : (c + 1) * step * tile],
                    columns(p, c),
                    preferred_element_type=jnp.float32,
                )
            give_ref[p, i] = (-total).T.astype(give_ref.dtype)
            o_copy(p, i).start()
            return carry

        lax.fori_loop(0, shares, block, 0)
        for i in range(shares):
            pending.append((lambda i=i: o_copy(p, i), None))

    def mine(s):
        first = row * 2 * shares + y * shares

        def block(i, carry):
            g = s * shares + i
            mine_load(g).wait()
            total = jnp.zeros((tile, tile), jnp.float32)
            for c in range(blocks // step):
                left = jnp.concatenate(
                    [
                        mine_ref[g % 2, :, j * tile : (j + 1) * tile] * gate_of(first + i, j)
                        for j in range(c * step, (c + 1) * step)
                    ],
                    axis=1,
                )
                right = jnp.concatenate(
                    [columns(s * halves + h, c) for h in range(halves)], axis=1
                )
                total += jnp.dot(left, right, preferred_element_type=jnp.float32)

            @pl.when(g + 2 < snodes * shares)
            def _():
                mine_load(g + 2).start()

            total = (-total).T
            rows = pl.ds(pl.multiple_of(i * tile, tile), tile)
            for h in range(halves):
                o_copy(s * halves + h, i).wait_recv()
                span = slice(h * LANES, (h + 1) * LANES)
                res_ref[s, span, rows] = (
                    total[span] + take_ref[s * halves + h, i].astype(jnp.float32)
                ).astype(res_ref.dtype)
            return carry

        lax.fori_loop(0, shares, block, 0)
        pltpu.make_async_copy(res_ref.at[s], out_ref.at[s], out_sem.at[s]).start()

    spread(0)
    for c in loads[2:]:
        c.wait()
    for p in range(1, phases):
        normalize(p)
    for p in range(1, phases):
        spread(p)
    climb(0)
    gate_theirs()
    relay(0)
    climb(1)
    sort(0)
    for p in range(phases):
        if p + 1 < phases:
            relay(p + 1)
        if p + 2 < phases:
            climb(p + 2)
        pass_on(p)
        if p >= 1:
            forwarded(p - 1)
            theirs(p - 1)
            if p % halves == 0:
                mine(p // halves - 1)
        if p + 1 < phases:
            sort(p + 1)
        crossed(p)
    forwarded(phases - 1)
    theirs(phases - 1)
    mine(snodes - 1)
    for s in range(snodes):
        pltpu.make_async_copy(res_ref.at[s], out_ref.at[s], out_sem.at[s]).wait()
    for make, cond in pending:
        guarded(cond, lambda: make().wait_send())


def fused(inverse, mask, ancestor_inverse, l_rows, diag_inverse, row_size):
    local_rows, local_cols = ancestor_inverse.shape
    snodes, tile = diag_inverse.shape[:2]
    held = l_rows.shape[1] // tile
    cfg = sizes(row_size, snodes, tile, held, local_rows, local_cols)
    phases, blocks, shares, depth = cfg["phases"], cfg["blocks"], cfg["shares"], cfg["depth"]
    quarter = tile // PARTS
    total = inverse.shape[1]
    half = shares * tile
    kind = ancestor_inverse.dtype
    dma = pltpu.SemaphoreType.DMA
    scratch = [pltpu.VMEM((total, quarter, LANES), kind) for _ in range(phases)]
    scratch += [
        pltpu.VMEM((half, local_cols), kind),
        pltpu.VMEM((2, tile, local_cols), kind),
        pltpu.VMEM(l_rows.shape, kind),
        pltpu.VMEM(diag_inverse.shape, kind),
        pltpu.VMEM((phases, PARTS, held, quarter, LANES), kind),
        pltpu.VMEM((phases, blocks, quarter, LANES), kind),
        pltpu.VMEM((phases, PARTS, blocks, quarter, LANES), kind),
        pltpu.VMEM((phases, shares, LANES, tile), kind),
        pltpu.VMEM((phases, shares, LANES, tile), kind),
        pltpu.VMEM((snodes, tile, half), kind),
        dma((phases, 3)),
        dma((phases, 3)),
        dma((phases, 5)),
        dma((phases, depth)),
        dma((phases,)),
        dma((phases,)),
        dma((phases, 2)),
        dma((phases, 2)),
        dma((phases, 2)),
        dma((phases, 2)),
        dma((phases, shares)),
        dma((phases, shares)),
        dma((shares,)),
        dma((2,)),
        dma((snodes, 2)),
        dma((snodes,)),
    ]
    smem = pl.BlockSpec(memory_space=pltpu.SMEM)
    anywhere = pl.BlockSpec(memory_space=pl.ANY)
    return pl.pallas_call(
        functools.partial(fused_kernel, cfg),
        out_shape=jax.ShapeDtypeStruct((snodes, tile, half), kind),
        in_specs=[smem, smem, anywhere, anywhere, anywhere],
        out_specs=anywhere,
        scratch_shapes=scratch,
        compiler_params=pltpu.CompilerParams(
            collective_id=0, has_side_effects=True, vmem_limit_bytes=67043328
        ),
        name="fused",
    )(inverse, mask, ancestor_inverse, l_rows, diag_inverse)


def fast(ancestor_inverse, fill_mask, block_order, l_rows, diag_inverse):
    packed = jnp.arange(block_order.shape[1], dtype=jnp.int32)
    inverse = jnp.sum(
        jnp.where(block_order[:, None, :] == packed[None, :, None], packed[None, None, :], 0), axis=2
    ).astype(jnp.int32)
    return fused(
        inverse, fill_mask, ancestor_inverse, l_rows, diag_inverse, lax.axis_size("row")
    )


def plain(ancestor_inverse, fill_mask, block_order, l_rows, diag_inverse):
    row_index = lax.axis_index("row")
    col_index = lax.axis_index("col")
    local_rows, local_cols = ancestor_inverse.shape
    snode_count, tile_size = diag_inverse.shape[:2]
    block_count = fill_mask.shape[0]
    row_blocks = local_rows // tile_size
    col_blocks = local_cols // tile_size
    normed = jnp.einsum(
        "sxy,syz->sxz", l_rows, diag_inverse, preferred_element_type=jnp.float32
    ).astype(jnp.bfloat16)
    wanted = col_index * col_blocks + jnp.arange(col_blocks, dtype=jnp.int32)
    everything = lax.all_gather(normed, ("row", "col"), axis=1, tiled=True)
    pieces = everything.reshape(snode_count, block_count, tile_size, tile_size)
    selector = (block_order[:, None, :] == wanted[None, :, None]).astype(jnp.bfloat16)
    columns = jnp.einsum(
        "saq,sqxy->saxy", selector, pieces, preferred_element_type=jnp.float32
    ).astype(jnp.bfloat16)
    stacked = columns.transpose(1, 2, 0, 3).reshape(local_cols, snode_count * tile_size)
    tile_gate = lax.dynamic_slice(
        fill_mask, (row_index * row_blocks, col_index * col_blocks), (row_blocks, col_blocks)
    ).astype(jnp.bfloat16)
    masked = (
        ancestor_inverse.reshape(row_blocks, tile_size, col_blocks, tile_size)
        * tile_gate[:, None, :, None]
    ).reshape(local_rows, local_cols)
    share_rows = local_rows // lax.axis_size("col")
    own_rows = lax.psum_scatter(
        (-jnp.dot(masked, stacked, preferred_element_type=jnp.float32)).astype(jnp.bfloat16),
        "col",
        scatter_dimension=0,
        tiled=True,
    ).astype(jnp.float32)
    return (
        own_rows.reshape(share_rows, snode_count, tile_size).transpose(1, 2, 0).astype(jnp.bfloat16)
    )


def per_device(ancestor_inverse, fill_mask, block_order, l_rows, diag_inverse):
    tile = diag_inverse.shape[1]
    col_size = lax.axis_size("col")
    if (
        col_size == 2
        and lax.axis_size("row") in (4, 8)
        and tile % LANES == 0
        and tile % (PARTS * 16) == 0
        and l_rows.shape[1] % tile == 0
        and ancestor_inverse.shape[0] % (col_size * tile) == 0
    ):
        return fast(ancestor_inverse, fill_mask, block_order, l_rows, diag_inverse)
    return plain(ancestor_inverse, fill_mask, block_order, l_rows, diag_inverse)


def solution(mesh):
    return jax.shard_map(
        per_device,
        mesh=mesh,
        in_specs=(
            P(("snode", "row"), "col"),
            P("snode", None),
            P("snode", None),
            P("snode", ("row", "col"), None),
            P("snode", None, None),
        ),
        out_specs=P("snode", None, ("row", "col")),
        check_vma=False,
    )
```

time: 215 us -> 177 us (0.82)
  Pallas kernels: 200 us -> 173 us
  waiting for transfers between devices: 3.79 us -> 0 us
  other arithmetic: 3.98 us -> 1.36 us
  matrix products: 2.5 us -> 0 us
    pallas_call x3 -> x1, Pallas kernels: 200 us -> 173 us  [fused(): pl.pallas_call(functools.partial(fused_kernel, cfg), out_shape=jax.ShapeD...]
    ppermute x1 -> x0, waiting for transfers between devices: 3.79 us -> none  [fast(): received = lax.ppermute(theirs, 'col', [(0, 1), (1, 0)])]
    convert_element_type x1 -> x0, other arithmetic: 3.16 us -> none  [fast(): total = (mine + received.astype(jnp.float32)).astype(jnp.bfloat16)]
    dot_general x1 -> x0, matrix products: 2.5 us -> none  [fast(): jnp.einsum('sxy,syz->sxz', l_rows, diag_inverse, preferred_element_type=j...]
  transfers between devices with their start and end apart: 1 -> 0, of which waited for: 1 -> 0; matrix products, arithmetic and copies ran while one was open for 0% -> 0% of each run, Pallas kernels for 11% -> 0%
where the time goes in v1:
time: 177 us
  Pallas kernels  173 us (98%)
  local copies, waits for them, and re-layouts  2.46 us (1%)
    pallas_call x1, Pallas kernels, fused(): pl.pallas_call(functools.partial(fused_kernel, cfg), out_shape=jax.ShapeD...  173 us

profile of v1, /device:TPU:0, one launch (start us, length us, event | category | flops | bytes accessed | tf_op | source)
XLA Modules:
  0.0 176.9 jit_solution(17022749637681097527)
XLA Ops:
  0.0 1.4 select_reduce_fusion.inv_ref
  1.4 173.1 %fused.1 = bf16[2,256,1280]{2,1,0:T(8,128)(2,1)} custom-call(s32[2,80]{1,0:T(2,128)} %select_reduce_fusion.inv_ref, s32[80,80]{1,0:T(8,128)} %mask_ref.1, bf16[2560,10240]{1,0:T(8,128)(2,1)} %a_ref.1, bf16[2,1280,256]{2,1,0:T(8,128)(2,1)} %l_ref.1, bf16[2,256,256]{2,1,0:T(8,128)(2,1)} %d_ref.1), custom_call_target="tpu_custom_call" | custom-call | tf_op jit(solution)/shard_map/fused/pallas_call | solution.py:432
  174.4 2.5 %copy.7 = bf16[2,256,1280]{2,1,0:T(8,128)(2,1)} copy(bf16[2,256,1280]{2,1,0:T(8,128)(2,1)} %fused.1) | data formatting | bytes 2621440

commit v2 on v1

--- a/solution.py
+++ b/solution.py
@@ -10,36 +10,30 @@
 MESH = pl.DeviceIdType.MESH
 LANES = 128
 PARTS = 4
+AWAY = (0, 0, 0, 0, 14, 16, 18, 10)
 
 
 def sizes(row_size, snodes, tile, held, local_rows, local_cols):
-    depth = row_size // 2
-    halves = tile // LANES
-    phases = snodes * halves
     blocks = local_cols // tile
-    away = [blocks // 4] * phases
-    away[0] = 0
-    away[-1] = blocks // 10
     return dict(
-        depth=depth,
-        halves=halves,
-        phases=phases,
+        depth=row_size // 2,
+        halves=tile // LANES,
+        phases=2 * snodes * (tile // LANES),
         snodes=snodes,
         tile=tile,
         held=held,
         blocks=blocks,
         shares=local_rows // (2 * tile),
-        away=away,
+        away=[blocks * n // 40 for n in AWAY],
     )
 
 
-def fused_kernel(
-    cfg, inv_ref, mask_ref, a_ref, l_ref, d_ref, out_ref, *rest
-):
+def fused_kernel(cfg, inv_ref, mask_ref, a_ref, l_ref, d_ref, out_ref, *rest):
     depth, halves, phases = cfg["depth"], cfg["halves"], cfg["phases"]
     snodes, tile, held = cfg["snodes"], cfg["tile"], cfg["held"]
     blocks, shares, away = cfg["blocks"], cfg["shares"], cfg["away"]
-    lanes = rest[:phases]
+    lanes, rest = rest[:phases], rest[phases:]
+    cols, rest = rest[:phases], rest[phases:]
     (
         theirs_ref,
         mine_ref,
@@ -47,10 +41,10 @@
         d_vm,
         own_ref,
         pick_ref,
-        cols_ref,
         give_ref,
         take_ref,
         res_ref,
+        part_ref,
         b_send,
         b_recv,
         c_send,
@@ -67,9 +61,10 @@
         m_sem,
         in_sem,
         out_sem,
-    ) = rest[phases:]
-    quarter = tile // PARTS
+    ) = rest
+    strip = tile // PARTS // 2
     plane = PARTS * held
+    final = phases // 2 - 1
 
     row = lax.axis_index("row")
     y = lax.axis_index("col")
@@ -119,11 +114,6 @@
             m_sem.at[g % 2],
         )
 
-    for i in range(shares):
-        theirs_load(i).start()
-    for g in range(2):
-        mine_load(g).start()
-
     barrier = pltpu.get_barrier_semaphore()
     for dev, _ in sides:
         pl.semaphore_signal(barrier, inc=1, device_id=dev, device_id_type=MESH)
@@ -133,13 +123,14 @@
         def _():
             pl.semaphore_signal(barrier, inc=1, device_id=at(z + dz, x, y), device_id_type=MESH)
 
-    def normalize(p):
-        s, h = p // halves, p % halves
+    def normalize(g):
+        s, h = g // halves, g % halves
         rows = jnp.dot(
             l_vm[s], d_vm[s, :, h * LANES : (h + 1) * LANES], preferred_element_type=jnp.float32
-        ).astype(own_ref.dtype)
-        own_ref[p] = rows.reshape(held, PARTS, quarter, LANES).transpose(1, 0, 2, 3)
-        lanes[p][pl.ds(slot, held)] = own_ref[p, me]
+        ).reshape(held, PARTS, 2, strip, LANES)
+        for u in range(2):
+            own_ref[2 * g + u] = rows[:, :, u].astype(own_ref.dtype).transpose(1, 0, 2, 3)
+            lanes[2 * g + u][pl.ds(slot, held)] = own_ref[2 * g + u, me]
 
     for c in loads[:2]:
         c.wait()
@@ -153,7 +144,7 @@
     def _():
         pl.semaphore_wait(barrier, len(sides) + min(2, depth - 1))
 
-    pending = []
+    pending = {}
 
     def remote(src, dst, send, recv, dev):
         return pltpu.make_async_remote_copy(
@@ -166,9 +157,13 @@
         else:
             pl.when(cond)(fn)
 
-    def start(make, cond=None):
+    def start(key, make, cond=None):
         guarded(cond, lambda: make().start())
-        pending.append((make, cond))
+        pending.setdefault(key, []).append((make, cond))
+
+    def drain(*key):
+        for make, cond in pending.pop(key, []):
+            guarded(cond, lambda make=make: make().wait_send())
 
     def b_copy(p, k):
         dev, lane = sides[k]
@@ -178,7 +173,7 @@
 
     def spread(p):
         for k in (2, 0, 1):
-            start(lambda k=k: b_copy(p, k))
+            start(("b", p), lambda k=k: b_copy(p, k))
 
     def c_copy(p, source, target, index):
         span = pl.ds(source * plane, plane)
@@ -194,73 +189,82 @@
         for k in range(3):
             b_copy(p, k).wait_recv()
         for n, dz in enumerate(reach):
-            start(lambda n=n, dz=dz: c_copy(p, z, z + dz, n), exists(dz))
+            start(("c", p), lambda n=n, dz=dz: c_copy(p, z, z + dz, n), exists(dz))
 
     def relay(p):
         if depth < 4:
             return
 
-        @pl.when(inner)
-        def _():
-            c_copy(p, far, near, len(reach)).wait_recv()
-
-        start(lambda: c_copy(p, far, near, len(reach)), inner)
+        def c_far():
+            return c_copy(p, far, near, len(reach))
+
+        guarded(inner if p == phases - 1 else None, lambda: c_far().wait_recv())
+        start(("c", p), c_far, inner)
 
     def climbed(p):
         for k in range(1, depth):
             source = (z + k) % depth
             cond = None
             if depth >= 4:
-                cond = jnp.logical_not(jnp.logical_and(inner, source == far))
-            guarded(cond, lambda: c_copy(p, source, z, 0).wait_recv())
+                cond = source != far
+                if p == phases - 1:
+                    cond = jnp.logical_or(cond, jnp.logical_not(inner))
+            guarded(cond, lambda source=source: c_copy(p, source, z, 0).wait_recv())
 
     def y_copy(p):
-        return remote(pick_ref.at[p], cols_ref.at[p, me], y_send.at[p], y_recv.at[p], to_y)
-
-    def x_copy(p, k):
+        return remote(pick_ref.at[p], cols[p].at[me], y_send.at[p], y_recv.at[p], to_y)
+
+    def pieces(p):
+        first, rest = away[p], blocks - 2 * away[p]
+        if not first:
+            return [(0, 0, blocks)]
+        return [(0, blocks - first, first)] + ([(first, first, rest)] if rest else [])
+
+    def x_copy(p, k, n):
         lane = (me, lane_y)[k]
-        span = pl.ds((z % 2) * away[p], blocks - away[p])
+        even, odd, size = pieces(p)[n]
+        span = pl.ds(even + (z % 2) * (odd - even), size)
         return remote(
-            cols_ref.at[p, lane, span],
-            cols_ref.at[p, lane, span],
-            x_send.at[p, k],
-            x_recv.at[p, k],
-            to_x,
+            cols[p].at[lane, span], cols[p].at[lane, span], x_send.at[p, k, n], x_recv.at[p, k, n], to_x
         )
+
+    def cross(p, k):
+        for n in range(len(pieces(p))):
+            start(("x", p), lambda n=n: x_copy(p, k, n))
 
     def f_copy(p, k):
         lane = (lane_x, lane_d)[k]
         span = pl.ds((z % 2) * (blocks - away[p]), away[p])
         return remote(
-            cols_ref.at[p, lane, span],
-            cols_ref.at[p, lane, span],
-            f_send.at[p, k],
-            f_recv.at[p, k],
-            pair,
+            cols[p].at[lane, span], cols[p].at[lane, span], f_send.at[p, k], f_recv.at[p, k], pair
         )
 
     def sort(p):
         climbed(p)
-        s = p // halves
+        s = p // (2 * halves)
 
         def pick(j, carry):
             pick_ref[p, j] = lanes[p][inv_ref[s, (1 - y) * blocks + j]]
-            cols_ref[p, me, j] = lanes[p][inv_ref[s, y * blocks + j]]
+            cols[p][me, j] = lanes[p][inv_ref[s, y * blocks + j]]
             return carry
 
         lax.fori_loop(0, blocks, pick, 0)
-        start(lambda: y_copy(p))
-        start(lambda: x_copy(p, 0))
+        start(("y", p), lambda: y_copy(p))
+        cross(p, 0)
 
     def pass_on(p):
         y_copy(p).wait_recv()
-        start(lambda: x_copy(p, 1))
+        cross(p, 1)
+
+    def forward(p, k):
+        if away[p]:
+            x_copy(p, k, 0).wait_recv()
+            start(("f", p), lambda: f_copy(p, k))
 
     def crossed(p):
         for k in range(2):
-            x_copy(p, k).wait_recv()
-            if away[p]:
-                start(lambda k=k: f_copy(p, k))
+            for n in range(1 if away[p] else 0, len(pieces(p))):
+                x_copy(p, k, n).wait_recv()
 
     def forwarded(p):
         if away[p]:
@@ -290,42 +294,80 @@
 
     step = max(n for n in range(1, 5) if blocks % n == 0)
 
-    def columns(p, c):
-        part = cols_ref[p, :, c * step : (c + 1) * step]
-        return part.transpose(1, 0, 2, 3).reshape(step * tile, LANES)
-
-    def o_copy(p, i):
-        return remote(give_ref.at[p, i], take_ref.at[p, i], o_send.at[p, i], o_recv.at[p, i], to_y)
-
-    def theirs(p):
+    def stacked(strips):
+        return jnp.stack(strips, axis=2).transpose(1, 0, 2, 3, 4).reshape(-1, LANES)
+
+    def columns(g, c):
+        js = slice(c * step, (c + 1) * step)
+        return stacked([cols[2 * g + u][:, js] for u in range(2)])
+
+    def o_copy(g, i):
+        return remote(give_ref.at[g, i], take_ref.at[g, i], o_send.at[g, i], o_recv.at[g, i], to_y)
+
+    def send_block(g, i, total):
+        give_ref[g, i] = (-total).T.astype(give_ref.dtype)
+        o_copy(g, i).start()
+
+    def sent_blocks(g, lo, hi):
+        for i in range(lo, hi):
+            pending.setdefault(("o", g), []).append((lambda i=i: o_copy(g, i), None))
+
+    def theirs(g, lo, hi):
         def block(i, carry):
             rows = pl.ds(pl.multiple_of(i * tile, tile), tile)
             total = jnp.zeros((tile, LANES), jnp.float32)
             for c in range(blocks // step):
                 total += jnp.dot(
                     theirs_ref[rows, c * step * tile : (c + 1) * step * tile],
-                    columns(p, c),
+                    columns(g, c),
                     preferred_element_type=jnp.float32,
                 )
-            give_ref[p, i] = (-total).T.astype(give_ref.dtype)
-            o_copy(p, i).start()
+            send_block(g, i, total)
             return carry
 
+        lax.fori_loop(lo, hi, block, 0)
+        sent_blocks(g, lo, hi)
+
+    def theirs_half(g, last):
+        side = 1 - x if last else x
+
+        def block(i, carry):
+            rows = pl.ds(pl.multiple_of(i * tile, tile), tile)
+            total = jnp.zeros((tile, LANES), jnp.float32)
+            for c in range(blocks // step):
+                js = range(c * step, (c + 1) * step)
+                left = jnp.concatenate(
+                    [
+                        theirs_ref[rows, pl.ds(pl.multiple_of(j * tile + side * LANES, LANES), LANES)]
+                        for j in js
+                    ],
+                    axis=1,
+                )
+                right = [
+                    cols[2 * g + u][pl.ds(side * 2, 2), c * step : (c + 1) * step] for u in range(2)
+                ]
+                total += jnp.dot(left, stacked(right), preferred_element_type=jnp.float32)
+            if last:
+                send_block(g, i, total + part_ref[rows])
+            else:
+                part_ref[rows] = total
+            return carry
+
         lax.fori_loop(0, shares, block, 0)
-        for i in range(shares):
-            pending.append((lambda i=i: o_copy(p, i), None))
-
-    def mine(s):
+        if last:
+            sent_blocks(g, 0, shares)
+
+    def mine(s, lo, hi):
         first = row * 2 * shares + y * shares
 
         def block(i, carry):
-            g = s * shares + i
-            mine_load(g).wait()
+            n = s * shares + i
+            mine_load(n).wait()
             total = jnp.zeros((tile, tile), jnp.float32)
             for c in range(blocks // step):
                 left = jnp.concatenate(
                     [
-                        mine_ref[g % 2, :, j * tile : (j + 1) * tile] * gate_of(first + i, j)
+                        mine_ref[n % 2, :, j * tile : (j + 1) * tile] * gate_of(first + i, j)
                         for j in range(c * step, (c + 1) * step)
                     ],
                     axis=1,
@@ -335,9 +377,9 @@
                 )
                 total += jnp.dot(left, right, preferred_element_type=jnp.float32)
 
-            @pl.when(g + 2 < snodes * shares)
+            @pl.when(n + 2 < snodes * shares)
             def _():
-                mine_load(g + 2).start()
+                mine_load(n + 2).start()
 
             total = (-total).T
             rows = pl.ds(pl.multiple_of(i * tile, tile), tile)
@@ -349,42 +391,90 @@
                 ).astype(res_ref.dtype)
             return carry
 
-        lax.fori_loop(0, shares, block, 0)
-        pltpu.make_async_copy(res_ref.at[s], out_ref.at[s], out_sem.at[s]).start()
+        lax.fori_loop(lo, hi, block, 0)
+        if hi == shares:
+            pltpu.make_async_copy(res_ref.at[s], out_ref.at[s], out_sem.at[s]).start()
 
     spread(0)
+    spread(1)
+    for i in range(shares):
+        theirs_load(i).start()
+    for n in range(2):
+        mine_load(n).start()
     for c in loads[2:]:
         c.wait()
-    for p in range(1, phases):
-        normalize(p)
-    for p in range(1, phases):
-        spread(p)
+    for g in range(1, phases // 2):
+        normalize(g)
+        spread(2 * g)
+        spread(2 * g + 1)
     climb(0)
     gate_theirs()
     relay(0)
     climb(1)
     sort(0)
-    for p in range(phases):
-        if p + 1 < phases:
-            relay(p + 1)
-        if p + 2 < phases:
-            climb(p + 2)
-        pass_on(p)
-        if p >= 1:
-            forwarded(p - 1)
-            theirs(p - 1)
-            if p % halves == 0:
-                mine(p // halves - 1)
-        if p + 1 < phases:
-            sort(p + 1)
-        crossed(p)
-    forwarded(phases - 1)
-    theirs(phases - 1)
-    mine(snodes - 1)
+    relay(1)
+    climb(2)
+    pass_on(0)
+    sort(1)
+    relay(2)
+    climb(3)
+    pass_on(1)
+    sort(2)
+    relay(3)
+    climb(4)
+    crossed(0)
+    crossed(1)
+    pass_on(2)
+    sort(3)
+    theirs(0, 0, 3)
+    relay(4)
+    climb(5)
+    theirs(0, 3, 5)
+    pass_on(3)
+    sort(4)
+    relay(5)
+    climb(6)
+    crossed(2)
+    pass_on(4)
+    sort(5)
+    relay(6)
+    climb(7)
+    crossed(3)
+    theirs(1, 0, 3)
+    pass_on(5)
+    theirs(1, 3, 5)
+    sort(6)
+    relay(7)
+    forward(4, 0)
+    forward(4, 1)
+    mine(0, 0, 3)
+    pass_on(6)
+    sort(7)
+    forward(5, 0)
+    mine(0, 3, 5)
+    forward(5, 1)
+    forward(6, 0)
+    crossed(4)
+    crossed(5)
+    pass_on(7)
+    forwarded(4)
+    forwarded(5)
+    theirs(2, 0, 3)
+    forward(6, 1)
+    theirs(2, 3, 5)
+    forward(7, 0)
+    theirs_half(final, False)
+    forward(7, 1)
+    crossed(6)
+    crossed(7)
+    forwarded(6)
+    forwarded(7)
+    theirs_half(final, True)
+    mine(1, 0, 5)
     for s in range(snodes):
         pltpu.make_async_copy(res_ref.at[s], out_ref.at[s], out_sem.at[s]).wait()
-    for make, cond in pending:
-        guarded(cond, lambda: make().wait_send())
+    for key in list(pending):
+        drain(*key)
 
 
 def fused(inverse, mask, ancestor_inverse, l_rows, diag_inverse, row_size):
@@ -393,35 +483,37 @@
     held = l_rows.shape[1] // tile
     cfg = sizes(row_size, snodes, tile, held, local_rows, local_cols)
     phases, blocks, shares, depth = cfg["phases"], cfg["blocks"], cfg["shares"], cfg["depth"]
-    quarter = tile // PARTS
+    strip = tile // PARTS // 2
+    groups = phases // 2
     total = inverse.shape[1]
     half = shares * tile
     kind = ancestor_inverse.dtype
     dma = pltpu.SemaphoreType.DMA
-    scratch = [pltpu.VMEM((total, quarter, LANES), kind) for _ in range(phases)]
+    scratch = [pltpu.VMEM((total, strip, LANES), kind) for _ in range(phases)]
+    scratch += [pltpu.VMEM((PARTS, blocks, strip, LANES), kind) for _ in range(phases)]
     scratch += [
         pltpu.VMEM((half, local_cols), kind),
         pltpu.VMEM((2, tile, local_cols), kind),
         pltpu.VMEM(l_rows.shape, kind),
         pltpu.VMEM(diag_inverse.shape, kind),
-        pltpu.VMEM((phases, PARTS, held, quarter, LANES), kind),
-        pltpu.VMEM((phases, blocks, quarter, LANES), kind),
-        pltpu.VMEM((phases, PARTS, blocks, quarter, LANES), kind),
-        pltpu.VMEM((phases, shares, LANES, tile), kind),
-        pltpu.VMEM((phases, shares, LANES, tile), kind),
+        pltpu.VMEM((phases, PARTS, held, strip, LANES), kind),
+        pltpu.VMEM((phases, blocks, strip, LANES), kind),
+        pltpu.VMEM((groups, shares, LANES, tile), kind),
+        pltpu.VMEM((groups, shares, LANES, tile), kind),
         pltpu.VMEM((snodes, tile, half), kind),
+        pltpu.VMEM((half, LANES), jnp.float32),
         dma((phases, 3)),
         dma((phases, 3)),
         dma((phases, 5)),
         dma((phases, depth)),
         dma((phases,)),
         dma((phases,)),
+        dma((phases, 2, 2)),
+        dma((phases, 2, 2)),
         dma((phases, 2)),
         dma((phases, 2)),
-        dma((phases, 2)),
-        dma((phases, 2)),
-        dma((phases, shares)),
-        dma((phases, shares)),
+        dma((groups, shares)),
+        dma((groups, shares)),
         dma((shares,)),
         dma((2,)),
         dma((snodes, 2)),
@@ -496,8 +588,8 @@
     if (
         col_size == 2
         and lax.axis_size("row") in (4, 8)
-        and tile % LANES == 0
-        and tile % (PARTS * 16) == 0
+        and tile == 2 * LANES
+        and diag_inverse.shape[0] == 2
         and l_rows.shape[1] % tile == 0
         and ancestor_inverse.shape[0] % (col_size * tile) == 0
     ):

time: 177 us -> 147 us (0.83)
  Pallas kernels: 173 us -> 143 us
    pallas_call x1, Pallas kernels: 173 us -> 143 us  [fused(): pl.pallas_call(functools.partial(fused_kernel, cfg), out_shape=jax.ShapeD...]
where the time goes in v2:
time: 147 us
  Pallas kernels  143 us (97%)
  local copies, waits for them, and re-layouts  2.46 us (2%)
    pallas_call x1, Pallas kernels, fused(): pl.pallas_call(functools.partial(fused_kernel, cfg), out_shape=jax.ShapeD...  143 us

profile of v2, /device:TPU:0, one launch (start us, length us, event | category | flops | bytes accessed | tf_op | source)
XLA Modules:
  0.0 147.0 jit_solution(1130249961793776618)
XLA Ops:
  0.0 1.4 select_reduce_fusion.inv_ref
  1.4 143.2 %fused.1 = bf16[2,256,1280]{2,1,0:T(8,128)(2,1)} custom-call(s32[2,80]{1,0:T(2,128)} %select_reduce_fusion.inv_ref, s32[80,80]{1,0:T(8,128)} %mask_ref.1, bf16[2560,10240]{1,0:T(8,128)(2,1)} %a_ref.1, bf16[2,1280,256]{2,1,0:T(8,128)(2,1)} %l_ref.1, bf16[2,256,256]{2,1,0:T(8,128)(2,1)} %d_ref.1), custom_call_target="tpu_custom_call" | custom-call | tf_op jit(solution)/shard_map/fused/pallas_call | solution.py:524
  144.5 2.5 %copy.7 = bf16[2,256,1280]{2,1,0:T(8,128)(2,1)} copy(bf16[2,256,1280]{2,1,0:T(8,128)(2,1)} %fused.1) | data formatting | bytes 2621440

commit v3 on v2

--- a/solution.py
+++ b/solution.py
@@ -28,7 +28,7 @@
     )
 
 
-def fused_kernel(cfg, inv_ref, mask_ref, a_ref, l_ref, d_ref, out_ref, *rest):
+def fused_kernel(cfg, order_hbm, mask_hbm, a_ref, l_ref, d_ref, out_ref, *rest):
     depth, halves, phases = cfg["depth"], cfg["halves"], cfg["phases"]
     snodes, tile, held = cfg["snodes"], cfg["tile"], cfg["held"]
     blocks, shares, away = cfg["blocks"], cfg["shares"], cfg["away"]
@@ -39,6 +39,10 @@
         mine_ref,
         l_vm,
         d_vm,
+        order_vm,
+        table_vm,
+        inv_ref,
+        mask_ref,
         own_ref,
         pick_ref,
         give_ref,
@@ -46,16 +50,15 @@
         res_ref,
         part_ref,
         b_send,
+        c_send,
+        y_send,
+        x_send,
+        o_send,
         b_recv,
-        c_send,
         c_recv,
-        y_send,
         y_recv,
-        x_send,
         x_recv,
-        f_send,
         f_recv,
-        o_send,
         o_recv,
         a_sem,
         m_sem,
@@ -64,7 +67,6 @@
     ) = rest
     strip = tile // PARTS // 2
     plane = PARTS * held
-    final = phases // 2 - 1
 
     row = lax.axis_index("row")
     y = lax.axis_index("col")
@@ -97,7 +99,10 @@
     for s in range(snodes):
         loads.append(pltpu.make_async_copy(l_ref.at[s], l_vm.at[s], in_sem.at[s, 0]))
         loads.append(pltpu.make_async_copy(d_ref.at[s], d_vm.at[s], in_sem.at[s, 1]))
-    for c in loads:
+    order_load = pltpu.make_async_copy(order_hbm, order_vm, in_sem.at[snodes, 0])
+    mask_load = pltpu.make_async_copy(mask_hbm, mask_ref, in_sem.at[snodes, 1])
+    table_move = pltpu.make_async_copy(table_vm, inv_ref, in_sem.at[snodes, 0])
+    for c in loads[:2] + [order_load] + loads[2:]:
         c.start()
 
     def theirs_load(i):
@@ -144,8 +149,6 @@
     def _():
         pl.semaphore_wait(barrier, len(sides) + min(2, depth - 1))
 
-    pending = {}
-
     def remote(src, dst, send, recv, dev):
         return pltpu.make_async_remote_copy(
             src_ref=src, dst_ref=dst, send_sem=send, recv_sem=recv, device_id=dev, device_id_type=MESH
@@ -157,62 +160,60 @@
         else:
             pl.when(cond)(fn)
 
-    def start(key, make, cond=None):
+    def start(make, cond=None):
         guarded(cond, lambda: make().start())
-        pending.setdefault(key, []).append((make, cond))
-
-    def drain(*key):
-        for make, cond in pending.pop(key, []):
-            guarded(cond, lambda make=make: make().wait_send())
+
+    def arrive(like, sem):
+        pltpu.make_async_copy(like, like, sem).wait()
 
     def b_copy(p, k):
         dev, lane = sides[k]
         return remote(
-            own_ref.at[p, lane], lanes[p].at[pl.ds(slot, held)], b_send.at[p, k], b_recv.at[p, k], dev
+            own_ref.at[p, lane], lanes[p].at[pl.ds(slot, held)], b_send, b_recv.at[p], dev
         )
 
     def spread(p):
         for k in (2, 0, 1):
-            start(("b", p), lambda k=k: b_copy(p, k))
+            start(lambda k=k: b_copy(p, k))
+
+    def far_of(zz):
+        return jnp.where(zz * 2 < depth, zz + 2, zz - 2)
 
     def c_copy(p, source, target, index):
         span = pl.ds(source * plane, plane)
+        kind = jnp.where(far_of(target) == source, 1, 0)
         return remote(
             lanes[p].at[span],
             lanes[p].at[span],
-            c_send.at[p, index],
-            c_recv.at[p, source],
+            c_send.at[index],
+            c_recv.at[p, kind],
             at(target, x, y),
         )
 
     def climb(p):
-        for k in range(3):
-            b_copy(p, k).wait_recv()
+        arrive(own_ref.at[p, 0:3], b_recv.at[p])
         for n, dz in enumerate(reach):
-            start(("c", p), lambda n=n, dz=dz: c_copy(p, z, z + dz, n), exists(dz))
+            start(lambda n=n, dz=dz: c_copy(p, z, z + dz, n), exists(dz))
+
+    def far_arrives(p):
+        arrive(lanes[p].at[0:plane], c_recv.at[p, 1])
 
     def relay(p):
         if depth < 4:
             return
-
-        def c_far():
-            return c_copy(p, far, near, len(reach))
-
-        guarded(inner if p == phases - 1 else None, lambda: c_far().wait_recv())
-        start(("c", p), c_far, inner)
+        guarded(inner if p == phases - 1 else None, lambda: far_arrives(p))
+        start(lambda: c_copy(p, far, near, len(reach)), inner)
 
     def climbed(p):
-        for k in range(1, depth):
-            source = (z + k) % depth
-            cond = None
-            if depth >= 4:
-                cond = source != far
-                if p == phases - 1:
-                    cond = jnp.logical_or(cond, jnp.logical_not(inner))
-            guarded(cond, lambda source=source: c_copy(p, source, z, 0).wait_recv())
+        others = depth - 1
+        if depth >= 4:
+            others -= 1
+            if p == phases - 1:
+                guarded(jnp.logical_not(inner), lambda: far_arrives(p))
+        arrive(lanes[p].at[0 : others * plane], c_recv.at[p, 0])
 
     def y_copy(p):
-        return remote(pick_ref.at[p], cols[p].at[me], y_send.at[p], y_recv.at[p], to_y)
+        return remote(pick_ref.at[p], cols[p].at[me], y_send, y_recv.at[p], to_y)
 
     def pieces(p):
         first, rest = away[p], blocks - 2 * away[p]
@@ -220,36 +221,40 @@
             return [(0, 0, blocks)]
         return [(0, blocks - first, first)] + ([(first, first, rest)] if rest else [])
 
+    def x_slot(p, kind):
+        before = sum(3 if away[n] else 1 for n in range(p))
+        return before + (kind if away[p] else 0)
+
     def x_copy(p, k, n):
         lane = (me, lane_y)[k]
         even, odd, size = pieces(p)[n]
         span = pl.ds(even + (z % 2) * (odd - even), size)
-        return remote(
-            cols[p].at[lane, span], cols[p].at[lane, span], x_send.at[p, k, n], x_recv.at[p, k, n], to_x
-        )
+        sem = x_recv.at[x_slot(p, k if away[p] and n == 0 else 2)]
+        return remote(cols[p].at[lane, span], cols[p].at[lane, span], x_send.at[k], sem, to_x)
 
     def cross(p, k):
         for n in range(len(pieces(p))):
-            start(("x", p), lambda n=n: x_copy(p, k, n))
+            start(lambda n=n: x_copy(p, k, n))
 
     def f_copy(p, k):
         lane = (lane_x, lane_d)[k]
         span = pl.ds((z % 2) * (blocks - away[p]), away[p])
-        return remote(
-            cols[p].at[lane, span], cols[p].at[lane, span], f_send.at[p, k], f_recv.at[p, k], pair
-        )
+        sem = f_recv.at[sum(1 for n in range(p) if away[n])]
+        return remote(cols[p].at[lane, span], cols[p].at[lane, span], x_send.at[k], sem, pair)
 
     def sort(p):
         climbed(p)
+        if p == 0:
+            table_move.wait()
         s = p // (2 * halves)
 
         def pick(j, carry):
-            pick_ref[p, j] = lanes[p][inv_ref[s, (1 - y) * blocks + j]]
-            cols[p][me, j] = lanes[p][inv_ref[s, y * blocks + j]]
+            pick_ref[p, j] = lanes[p][inv_ref[s, (1 - y) * blocks + j, 0]]
+            cols[p][me, j] = lanes[p][inv_ref[s, y * blocks + j, 0]]
             return carry
 
         lax.fori_loop(0, blocks, pick, 0)
-        start(("y", p), lambda: y_copy(p))
+        start(lambda: y_copy(p))
         cross(p, 0)
 
     def pass_on(p):
@@ -258,18 +263,31 @@
 
     def forward(p, k):
         if away[p]:
-            x_copy(p, k, 0).wait_recv()
-            start(("f", p), lambda: f_copy(p, k))
+            arrive(cols[p].at[0, 0 : away[p]], x_recv.at[x_slot(p, k)])
+            start(lambda: f_copy(p, k))
 
     def crossed(p):
-        for k in range(2):
-            for n in range(1 if away[p] else 0, len(pieces(p))):
-                x_copy(p, k, n).wait_recv()
+        size = blocks - 2 * away[p]
+        if size:
+            arrive(cols[p].at[0:2, 0:size], x_recv.at[x_slot(p, 2)])
 
     def forwarded(p):
         if away[p]:
-            for k in range(2):
-                f_copy(p, k).wait_recv()
+            arrive(cols[p].at[0:2, 0 : away[p]], f_copy_sem(p))
+
+    def f_copy_sem(p):
+        return f_recv.at[sum(1 for n in range(p) if away[n])]
+
+    def make_table():
+        order_load.wait()
+        shape = (inv_ref.shape[1], order_hbm.shape[1])
+        wanted = lax.broadcasted_iota(jnp.int32, shape, 0)
+        packed = lax.broadcasted_iota(jnp.int32, shape, 1)
+        for s in range(snodes):
+            found = jnp.where(order_vm[s : s + 1, :] == wanted, packed, 0)
+            place = jnp.max(found, axis=1, keepdims=True)
+            table_vm[s] = jnp.broadcast_to(place, table_vm.shape[1:])
+        table_move.start()
 
     def gate_of(i, j):
         return mask_ref[i, y * blocks + j].astype(jnp.float32).astype(theirs_ref.dtype)
@@ -293,6 +311,7 @@
         lax.fori_loop(0, shares, one_row, 0)
 
     step = max(n for n in range(1, 5) if blocks % n == 0)
+    wide = max(n for n in range(1, 9) if blocks % n == 0)
 
     def stacked(strips):
         return jnp.stack(strips, axis=2).transpose(1, 0, 2, 3, 4).reshape(-1, LANES)
@@ -302,15 +321,13 @@
         return stacked([cols[2 * g + u][:, js] for u in range(2)])
 
     def o_copy(g, i):
-        return remote(give_ref.at[g, i], take_ref.at[g, i], o_send.at[g, i], o_recv.at[g, i], to_y)
+        return remote(
+            give_ref.at[g, i], take_ref.at[g, i], o_send, o_recv.at[g // halves, i], to_y
+        )
 
     def send_block(g, i, total):
         give_ref[g, i] = (-total).T.astype(give_ref.dtype)
         o_copy(g, i).start()
-
-    def sent_blocks(g, lo, hi):
-        for i in range(lo, hi):
-            pending.setdefault(("o", g), []).append((lambda i=i: o_copy(g, i), None))
 
     def theirs(g, lo, hi):
         def block(i, carry):
@@ -326,48 +343,74 @@
             return carry
 
         lax.fori_loop(lo, hi, block, 0)
-        sent_blocks(g, lo, hi)
-
-    def theirs_half(g, last):
-        side = 1 - x if last else x
-
+
+    def side_dot(groups, side, rows):
+        total = jnp.zeros((tile, len(groups) * LANES), jnp.float32)
+        for c in range(blocks // wide):
+            left = jnp.concatenate(
+                [
+                    theirs_ref[rows, pl.ds(pl.multiple_of(j * tile + side * LANES, LANES), LANES)]
+                    for j in range(c * wide, (c + 1) * wide)
+                ],
+                axis=1,
+            )
+            right = [
+                stacked(
+                    [cols[2 * g + u][pl.ds(side * 2, 2), c * wide : (c + 1) * wide] for u in range(2)]
+                )
+                for g in groups
+            ]
+            total += jnp.dot(
+                left, jnp.concatenate(right, axis=1), preferred_element_type=jnp.float32
+            )
+        return total
+
+    def theirs_near(groups):
         def block(i, carry):
             rows = pl.ds(pl.multiple_of(i * tile, tile), tile)
-            total = jnp.zeros((tile, LANES), jnp.float32)
-            for c in range(blocks // step):
-                js = range(c * step, (c + 1) * step)
-                left = jnp.concatenate(
-                    [
-                        theirs_ref[rows, pl.ds(pl.multiple_of(j * tile + side * LANES, LANES), LANES)]
-                        for j in js
-                    ],
-                    axis=1,
-                )
-                right = [
-                    cols[2 * g + u][pl.ds(side * 2, 2), c * step : (c + 1) * step] for u in range(2)
-                ]
-                total += jnp.dot(left, stacked(right), preferred_element_type=jnp.float32)
-            if last:
-                send_block(g, i, total + part_ref[rows])
-            else:
-                part_ref[rows] = total
+            part_ref[rows, : len(groups) * LANES] = side_dot(groups, x, rows)
             return carry
 
         lax.fori_loop(0, shares, block, 0)
-        if last:
-            sent_blocks(g, 0, shares)
-
-    def mine(s, lo, hi):
+
+    def theirs_far(g, n):
+        def block(i, carry):
+            rows = pl.ds(pl.multiple_of(i * tile, tile), tile)
+            total = side_dot([g], 1 - x, rows)
+            send_block(g, i, total + part_ref[rows, n * LANES : (n + 1) * LANES])
+            if g == phases // 2 - 1:
+
+                @pl.when(i + 2 < shares)
+                def _():
+                    late_load(i).start()
+
+            return carry
+
+        lax.fori_loop(0, shares, block, 0)
+
+    def late_load(i):
+        return pltpu.make_async_copy(
+            a_ref.at[pl.ds((y * shares + 2 + i) * tile, tile)],
+            theirs_ref.at[pl.ds(i * tile, tile)],
+            a_sem.at[i],
+        )
+
+    def mine(s, lo, hi, late=False):
         first = row * 2 * shares + y * shares
 
         def block(i, carry):
             n = s * shares + i
-            mine_load(n).wait()
+            if late:
+                late_load(i - 2).wait()
+                source = theirs_ref.at[pl.ds(pl.multiple_of((i - 2) * tile, tile), tile)]
+            else:
+                mine_load(n).wait()
+                source = mine_ref.at[n % 2]
             total = jnp.zeros((tile, tile), jnp.float32)
             for c in range(blocks // step):
                 left = jnp.concatenate(
                     [
-                        mine_ref[n % 2, :, j * tile : (j + 1) * tile] * gate_of(first + i, j)
+                        source[:, j * tile : (j + 1) * tile] * gate_of(first + i, j)
                         for j in range(c * step, (c + 1) * step)
                     ],
                     axis=1,
@@ -377,26 +420,28 @@
                 )
                 total += jnp.dot(left, right, preferred_element_type=jnp.float32)
 
-            @pl.when(n + 2 < snodes * shares)
-            def _():
+            if s == 0:
                 mine_load(n + 2).start()
 
             total = (-total).T
             rows = pl.ds(pl.multiple_of(i * tile, tile), tile)
+            both = pl.ds(s * halves, halves)
+            arrive(take_ref.at[both, i], o_recv.at[s, i])
             for h in range(halves):
-                o_copy(s * halves + h, i).wait_recv()
                 span = slice(h * LANES, (h + 1) * LANES)
                 res_ref[s, span, rows] = (
                     total[span] + take_ref[s * halves + h, i].astype(jnp.float32)
                 ).astype(res_ref.dtype)
+            pltpu.make_async_copy(
+                res_ref.at[s, :, rows], out_ref.at[s, :, rows], out_sem.at[s]
+            ).start()
             return carry
 
         lax.fori_loop(lo, hi, block, 0)
-        if hi == shares:
-            pltpu.make_async_copy(res_ref.at[s], out_ref.at[s], out_sem.at[s]).start()
 
     spread(0)
     spread(1)
+    mask_load.start()
     for i in range(shares):
         theirs_load(i).start()
     for n in range(2):
@@ -408,6 +453,8 @@
         spread(2 * g)
         spread(2 * g + 1)
     climb(0)
+    make_table()
+    mask_load.wait()
     gate_theirs()
     relay(0)
     climb(1)
@@ -435,14 +482,14 @@
     relay(5)
     climb(6)
     crossed(2)
+    theirs_near([1])
     pass_on(4)
     sort(5)
     relay(6)
     climb(7)
     crossed(3)
-    theirs(1, 0, 3)
+    theirs_far(1, 0)
     pass_on(5)
-    theirs(1, 3, 5)
     sort(6)
     relay(7)
     forward(4, 0)
@@ -451,33 +498,40 @@
     pass_on(6)
     sort(7)
     forward(5, 0)
+    forward(5, 1)
     mine(0, 3, 5)
-    forward(5, 1)
     forward(6, 0)
     crossed(4)
     crossed(5)
     pass_on(7)
+    forward(6, 1)
+    theirs_near([2, 3])
+    forward(7, 0)
+    forward(7, 1)
     forwarded(4)
     forwarded(5)
-    theirs(2, 0, 3)
-    forward(6, 1)
-    theirs(2, 3, 5)
-    forward(7, 0)
-    theirs_half(final, False)
-    forward(7, 1)
+    theirs_far(2, 0)
     crossed(6)
     crossed(7)
     forwarded(6)
     forwarded(7)
-    theirs_half(final, True)
-    mine(1, 0, 5)
+    theirs_far(3, 1)
+    mine(1, 0, 2)
+    mine(1, 2, 5, True)
     for s in range(snodes):
         pltpu.make_async_copy(res_ref.at[s], out_ref.at[s], out_sem.at[s]).wait()
-    for key in list(pending):
-        drain(*key)
-
-
-def fused(inverse, mask, ancestor_inverse, l_rows, diag_inverse, row_size):
+    arrive(own_ref.at[:, 0:3], b_send)
+    for n, dz in enumerate(reach):
+        guarded(exists(dz), lambda n=n: arrive(own_ref, c_send.at[n]))
+    if depth >= 4:
+        guarded(inner, lambda: arrive(own_ref, c_send.at[len(reach)]))
+    arrive(pick_ref, y_send)
+    for k in range(2):
+        arrive(pick_ref, x_send.at[k])
+    arrive(give_ref, o_send)
+
+
+def fused(order, mask, ancestor_inverse, l_rows, diag_inverse, row_size):
     local_rows, local_cols = ancestor_inverse.shape
     snodes, tile = diag_inverse.shape[:2]
     held = l_rows.shape[1] // tile
@@ -485,7 +539,9 @@
     phases, blocks, shares, depth = cfg["phases"], cfg["blocks"], cfg["shares"], cfg["depth"]
     strip = tile // PARTS // 2
     groups = phases // 2
-    total = inverse.shape[1]
+    halves = cfg["halves"]
+    away = cfg["away"]
+    total = order.shape[1]
     half = shares * tile
     kind = ancestor_inverse.dtype
     dma = pltpu.SemaphoreType.DMA
@@ -496,51 +552,49 @@
         pltpu.VMEM((2, tile, local_cols), kind),
         pltpu.VMEM(l_rows.shape, kind),
         pltpu.VMEM(diag_inverse.shape, kind),
+        pltpu.VMEM(order.shape, jnp.int32),
+        pltpu.VMEM((snodes, total, LANES), jnp.int32),
+        pltpu.SMEM((snodes, total, LANES), jnp.int32),
+        pltpu.SMEM(mask.shape, jnp.int32),
         pltpu.VMEM((phases, PARTS, held, strip, LANES), kind),
         pltpu.VMEM((phases, blocks, strip, LANES), kind),
         pltpu.VMEM((groups, shares, LANES, tile), kind),
         pltpu.VMEM((groups, shares, LANES, tile), kind),
         pltpu.VMEM((snodes, tile, half), kind),
-        pltpu.VMEM((half, LANES), jnp.float32),
-        dma((phases, 3)),
-        dma((phases, 3)),
-        dma((phases, 5)),
-        dma((phases, depth)),
+        pltpu.VMEM((half, halves * LANES), jnp.float32),
+        dma,
+        dma((5,)),
+        dma,
+        dma((2,)),
+        dma,
         dma((phases,)),
+        dma((phases, 2)),
         dma((phases,)),
-        dma((phases, 2, 2)),
-        dma((phases, 2, 2)),
-        dma((phases, 2)),
-        dma((phases, 2)),
-        dma((groups, shares)),
-        dma((groups, shares)),
+        dma((sum(3 if n else 1 for n in away),)),
+        dma((max(1, sum(1 for n in away if n)),)),
+        dma((snodes, shares)),
         dma((shares,)),
         dma((2,)),
-        dma((snodes, 2)),
+        dma((snodes + 1, 2)),
         dma((snodes,)),
     ]
-    smem = pl.BlockSpec(memory_space=pltpu.SMEM)
     anywhere = pl.BlockSpec(memory_space=pl.ANY)
     return pl.pallas_call(
         functools.partial(fused_kernel, cfg),
         out_shape=jax.ShapeDtypeStruct((snodes, tile, half), kind),
-        in_specs=[smem, smem, anywhere, anywhere, anywhere],
+        in_specs=[anywhere] * 5,
         out_specs=anywhere,
         scratch_shapes=scratch,
         compiler_params=pltpu.CompilerParams(
             collective_id=0, has_side_effects=True, vmem_limit_bytes=67043328
         ),
         name="fused",
-    )(inverse, mask, ancestor_inverse, l_rows, diag_inverse)
+    )(order, mask, ancestor_inverse, l_rows, diag_inverse)
 
 
 def fast(ancestor_inverse, fill_mask, block_order, l_rows, diag_inverse):
-    packed = jnp.arange(block_order.shape[1], dtype=jnp.int32)
-    inverse = jnp.sum(
-        jnp.where(block_order[:, None, :] == packed[None, :, None], packed[None, None, :], 0), axis=2
-    ).astype(jnp.int32)
     return fused(
-        inverse, fill_mask, ancestor_inverse, l_rows, diag_inverse, lax.axis_size("row")
+        block_order, fill_mask, ancestor_inverse, l_rows, diag_inverse, lax.axis_size("row")
     )
 
 

time: 147 us -> 136 us (0.925)
  Pallas kernels: 143 us -> 133 us
    pallas_call x1, Pallas kernels: 143 us -> 133 us  [fused(): pl.pallas_call(functools.partial(fused_kernel, cfg), out_shape=jax.ShapeD...]
where the time goes in v3:
time: 136 us; the launch traced here: 135 us
  Pallas kernels  133 us (98%)
  local copies, waits for them, and re-layouts  2.46 us (2%)
    pallas_call x1, Pallas kernels, fused(): pl.pallas_call(functools.partial(fused_kernel, cfg), out_shape=jax.ShapeD...  133 us

profile of v3, /device:TPU:0, one launch (start us, length us, event | category | flops | bytes accessed | tf_op | source)
XLA Modules:
  0.0 135.5 jit_solution(17627730777465594187)
XLA Ops:
  0.0 133.0 %fused.1 = bf16[2,256,1280]{2,1,0:T(8,128)(2,1)} custom-call(s32[2,80]{1,0:T(2,128)} %order_hbm.1, s32[80,80]{1,0:T(8,128)} %mask_hbm.1, bf16[2560,10240]{1,0:T(8,128)(2,1)} %a_ref.1, bf16[2,1280,256]{2,1,0:T(8,128)(2,1)} %l_ref.1, bf16[2,256,256]{2,1,0:T(8,128)(2,1)} %d_ref.1), custom_call_target="tpu_custom_call" | custom-call | tf_op jit(solution)/shard_map/fused/pallas_call | solution.py:582
  133.0 2.5 %copy.7 = bf16[2,256,1280]{2,1,0:T(8,128)(2,1)} copy(bf16[2,256,1280]{2,1,0:T(8,128)(2,1)} %fused.1) | data formatting | bytes 2621440

commit v4 on v3

--- a/solution.py
+++ b/solution.py
@@ -10,7 +10,8 @@
 MESH = pl.DeviceIdType.MESH
 LANES = 128
 PARTS = 4
-AWAY = (0, 0, 0, 0, 14, 16, 18, 10)
+AWAY = (0, 0, 0, 0, 16, 18, 20, 0)
+PICKS = 2
 
 
 def sizes(row_size, snodes, tile, held, local_rows, local_cols):
@@ -18,7 +19,7 @@
     return dict(
         depth=row_size // 2,
         halves=tile // LANES,
-        phases=2 * snodes * (tile // LANES),
+        spans=[(b, 0, tile // PARTS // 2) for b in range(2 * snodes * (tile // LANES))],
         snodes=snodes,
         tile=tile,
         held=held,
@@ -29,15 +30,15 @@
 
 
 def fused_kernel(cfg, order_hbm, mask_hbm, a_ref, l_ref, d_ref, out_ref, *rest):
-    depth, halves, phases = cfg["depth"], cfg["halves"], cfg["phases"]
+    depth, halves, spans = cfg["depth"], cfg["halves"], cfg["spans"]
+    phases, buffers = len(spans), spans[-1][0] + 1
     snodes, tile, held = cfg["snodes"], cfg["tile"], cfg["held"]
     blocks, shares, away = cfg["blocks"], cfg["shares"], cfg["away"]
     lanes, rest = rest[:phases], rest[phases:]
-    cols, rest = rest[:phases], rest[phases:]
+    cols, rest = rest[:buffers], rest[buffers:]
     (
         theirs_ref,
         mine_ref,
-        l_vm,
         d_vm,
         order_vm,
         table_vm,
@@ -49,6 +50,7 @@
         take_ref,
         res_ref,
         part_ref,
+        mine_part_ref,
         b_send,
         c_send,
         y_send,
@@ -95,9 +97,12 @@
     far = jnp.where(low, z + 2, z - 2)
     near = jnp.where(low, z - 1, z + 1)
 
+    def packed(s):
+        return theirs_ref.at[0 : held * tile, s * tile : (s + 1) * tile]
+
     loads = []
     for s in range(snodes):
-        loads.append(pltpu.make_async_copy(l_ref.at[s], l_vm.at[s], in_sem.at[s, 0]))
+        loads.append(pltpu.make_async_copy(l_ref.at[s], packed(s), in_sem.at[s, 0]))
         loads.append(pltpu.make_async_copy(d_ref.at[s], d_vm.at[s], in_sem.at[s, 1]))
     order_load = pltpu.make_async_copy(order_hbm, order_vm, in_sem.at[snodes, 0])
     mask_load = pltpu.make_async_copy(mask_hbm, mask_ref, in_sem.at[snodes, 1])
@@ -112,11 +117,11 @@
             a_sem.at[i],
         )
 
-    def mine_load(g):
+    def mine_load(n):
+        again = 2 * shares - 1
+        i = jnp.where(n < shares, n, jnp.where(n < again, n - shares, n - again))
         return pltpu.make_async_copy(
-            a_ref.at[pl.ds((y * shares + g % shares) * tile, tile)],
-            mine_ref.at[g % 2],
-            m_sem.at[g % 2],
+            a_ref.at[pl.ds((y * shares + i) * tile, tile)], mine_ref.at[n % 2], m_sem.at[n % 2]
         )
 
     barrier = pltpu.get_barrier_semaphore()
@@ -131,11 +136,14 @@
     def normalize(g):
         s, h = g // halves, g % halves
         rows = jnp.dot(
-            l_vm[s], d_vm[s, :, h * LANES : (h + 1) * LANES], preferred_element_type=jnp.float32
+            theirs_ref[0 : held * tile, s * tile : (s + 1) * tile],
+            d_vm[s, :, h * LANES : (h + 1) * LANES], preferred_element_type=jnp.float32
         ).reshape(held, PARTS, 2, strip, LANES)
         for u in range(2):
             own_ref[2 * g + u] = rows[:, :, u].astype(own_ref.dtype).transpose(1, 0, 2, 3)
-            lanes[2 * g + u][pl.ds(slot, held)] = own_ref[2 * g + u, me]
+            for p, (b, at_row, size) in enumerate(spans):
+                if b == 2 * g + u:
+                    lanes[p][pl.ds(slot, held)] = own_ref[b, me, :, at_row : at_row + size]
 
     for c in loads[:2]:
         c.wait()
@@ -166,10 +174,22 @@
     def arrive(like, sem):
         pltpu.make_async_copy(like, like, sem).wait()
 
+    def part_of(p):
+        b, at_row, size = spans[p]
+        return b, slice(at_row, at_row + size)
+
+    def strips(p, lane, span):
+        b, part = part_of(p)
+        return cols[b].at[lane, span, part]
+
+    def picked(p):
+        return pick_ref.at[p % PICKS]
+
     def b_copy(p, k):
         dev, lane = sides[k]
+        b, part = part_of(p)
         return remote(
-            own_ref.at[p, lane], lanes[p].at[pl.ds(slot, held)], b_send, b_recv.at[p], dev
+            own_ref.at[b, lane, :, part], lanes[p].at[pl.ds(slot, held)], b_send, b_recv.at[p], dev
         )
 
     def spread(p):
@@ -191,7 +211,8 @@
         )
 
     def climb(p):
-        arrive(own_ref.at[p, 0:3], b_recv.at[p])
+        b, part = part_of(p)
+        arrive(own_ref.at[b, 0:3, :, part], b_recv.at[p])
         for n, dz in enumerate(reach):
             start(lambda n=n, dz=dz: c_copy(p, z, z + dz, n), exists(dz))
 
@@ -213,7 +234,9 @@
         arrive(lanes[p].at[0 : others * plane], c_recv.at[p, 0])
 
     def y_copy(p):
-        return remote(pick_ref.at[p], cols[p].at[me], y_send, y_recv.at[p], to_y)
+        return remote(
+            picked(p), strips(p, me, slice(0, blocks)), y_send.at[p % PICKS], y_recv.at[p], to_y
+        )
 
     def pieces(p):
         first, rest = away[p], blocks - 2 * away[p]
@@ -230,7 +253,7 @@
         even, odd, size = pieces(p)[n]
         span = pl.ds(even + (z % 2) * (odd - even), size)
         sem = x_recv.at[x_slot(p, k if away[p] and n == 0 else 2)]
-        return remote(cols[p].at[lane, span], cols[p].at[lane, span], x_send.at[k], sem, to_x)
+        return remote(strips(p, lane, span), strips(p, lane, span), x_send.at[k], sem, to_x)
 
     def cross(p, k):
         for n in range(len(pieces(p))):
@@ -240,17 +263,21 @@
         lane = (lane_x, lane_d)[k]
         span = pl.ds((z % 2) * (blocks - away[p]), away[p])
         sem = f_recv.at[sum(1 for n in range(p) if away[n])]
-        return remote(cols[p].at[lane, span], cols[p].at[lane, span], x_send.at[k], sem, pair)
+        return remote(strips(p, lane, span), strips(p, lane, span), x_send.at[k], sem, pair)
 
     def sort(p):
         climbed(p)
         if p == 0:
             table_move.wait()
-        s = p // (2 * halves)
+        b, part = part_of(p)
+        s = b // (2 * halves)
+
+        if p >= PICKS:
+            arrive(picked(p), y_send.at[p % PICKS])
 
         def pick(j, carry):
-            pick_ref[p, j] = lanes[p][inv_ref[s, (1 - y) * blocks + j, 0]]
-            cols[p][me, j] = lanes[p][inv_ref[s, y * blocks + j, 0]]
+            pick_ref[p % PICKS, j] = lanes[p][inv_ref[s, (1 - y) * blocks + j, 0]]
+            cols[b][me, j, part] = lanes[p][inv_ref[s, y * blocks + j, 0]]
             return carry
 
         lax.fori_loop(0, blocks, pick, 0)
@@ -263,17 +290,17 @@
 
     def forward(p, k):
         if away[p]:
-            arrive(cols[p].at[0, 0 : away[p]], x_recv.at[x_slot(p, k)])
+            arrive(strips(p, 0, slice(0, away[p])), x_recv.at[x_slot(p, k)])
             start(lambda: f_copy(p, k))
 
     def crossed(p):
         size = blocks - 2 * away[p]
         if size:
-            arrive(cols[p].at[0:2, 0:size], x_recv.at[x_slot(p, 2)])
+            arrive(strips(p, slice(0, 2), slice(0, size)), x_recv.at[x_slot(p, 2)])
 
     def forwarded(p):
         if away[p]:
-            arrive(cols[p].at[0:2, 0 : away[p]], f_copy_sem(p))
+            arrive(strips(p, slice(0, 2), slice(0, away[p])), f_copy_sem(p))
 
     def f_copy_sem(p):
         return f_recv.at[sum(1 for n in range(p) if away[n])]
@@ -292,13 +319,11 @@
     def gate_of(i, j):
         return mask_ref[i, y * blocks + j].astype(jnp.float32).astype(theirs_ref.dtype)
 
-    def gate_theirs():
+    def gate(lo, hi):
         first = row * 2 * shares + (1 - y) * shares
 
         def one_row(i, carry):
-            pltpu.make_async_copy(
-                a_ref.at[pl.ds(0, tile)], theirs_ref.at[pl.ds(i * tile, tile)], a_sem.at[i]
-            ).wait()
+            arrive(theirs_ref.at[pl.ds(i * tile, tile)], a_sem.at[i])
             rows = pl.ds(pl.multiple_of(i * tile, tile), tile)
 
             def one(j, carry):
@@ -308,7 +333,7 @@
 
             return lax.fori_loop(0, blocks, one, carry)
 
-        lax.fori_loop(0, shares, one_row, 0)
+        lax.fori_loop(lo, hi, one_row, 0)
 
     step = max(n for n in range(1, 5) if blocks % n == 0)
     wide = max(n for n in range(1, 9) if blocks % n == 0)
@@ -344,12 +369,12 @@
 
         lax.fori_loop(lo, hi, block, 0)
 
-    def side_dot(groups, side, rows):
+    def side_dot(groups, side, left_of):
         total = jnp.zeros((tile, len(groups) * LANES), jnp.float32)
         for c in range(blocks // wide):
             left = jnp.concatenate(
                 [
-                    theirs_ref[rows, pl.ds(pl.multiple_of(j * tile + side * LANES, LANES), LANES)]
+                    left_of(j, pl.ds(pl.multiple_of(j * tile + side * LANES, LANES), LANES))
                     for j in range(c * wide, (c + 1) * wide)
                 ],
                 axis=1,
@@ -368,7 +393,7 @@
     def theirs_near(groups):
         def block(i, carry):
             rows = pl.ds(pl.multiple_of(i * tile, tile), tile)
-            part_ref[rows, : len(groups) * LANES] = side_dot(groups, x, rows)
+            part_ref[rows, : len(groups) * LANES] = side_dot(groups, x, lambda j, span: theirs_ref[rows, span])
             return carry
 
         lax.fori_loop(0, shares, block, 0)
@@ -376,9 +401,9 @@
     def theirs_far(g, n):
         def block(i, carry):
             rows = pl.ds(pl.multiple_of(i * tile, tile), tile)
-            total = side_dot([g], 1 - x, rows)
+            total = side_dot([g], 1 - x, lambda j, span: theirs_ref[rows, span])
             send_block(g, i, total + part_ref[rows, n * LANES : (n + 1) * LANES])
-            if g == phases // 2 - 1:
+            if g == buffers // 2 - 1:
 
                 @pl.when(i + 2 < shares)
                 def _():
@@ -395,22 +420,31 @@
             a_sem.at[i],
         )
 
-    def mine(s, lo, hi, late=False):
-        first = row * 2 * shares + y * shares
-
+    def finish(s, i, total):
+        total = (-total).T
+        rows = pl.ds(pl.multiple_of(i * tile, tile), tile)
+        both = pl.ds(s * halves, halves)
+        arrive(take_ref.at[both, i], o_recv.at[s, i])
+        for h in range(halves):
+            span = slice(h * LANES, (h + 1) * LANES)
+            res_ref[s, span, rows] = (
+                total[span] + take_ref[s * halves + h, i].astype(jnp.float32)
+            ).astype(res_ref.dtype)
+        pltpu.make_async_copy(
+            res_ref.at[s, :, rows], out_ref.at[s, :, rows], out_sem.at[s]
+        ).start()
+
+    first_mine = row * 2 * shares + y * shares
+
+    def mine(s, lo, hi):
         def block(i, carry):
-            n = s * shares + i
-            if late:
-                late_load(i - 2).wait()
-                source = theirs_ref.at[pl.ds(pl.multiple_of((i - 2) * tile, tile), tile)]
-            else:
-                mine_load(n).wait()
-                source = mine_ref.at[n % 2]
+            n = i
+            mine_load(n).wait()
             total = jnp.zeros((tile, tile), jnp.float32)
             for c in range(blocks // step):
                 left = jnp.concatenate(
                     [
-                        source[:, j * tile : (j + 1) * tile] * gate_of(first + i, j)
+                        mine_ref[n % 2, :, j * tile : (j + 1) * tile] * gate_of(first_mine + i, j)
                         for j in range(c * step, (c + 1) * step)
                     ],
                     axis=1,
@@ -419,48 +453,74 @@
                     [columns(s * halves + h, c) for h in range(halves)], axis=1
                 )
                 total += jnp.dot(left, right, preferred_element_type=jnp.float32)
-
-            if s == 0:
-                mine_load(n + 2).start()
-
-            total = (-total).T
+            mine_load(n + 2).start()
+            finish(s, i, total)
+            return carry
+
+        lax.fori_loop(lo, hi, block, 0)
+
+    tail = snodes - 1
+    tail_groups = [tail * halves + h for h in range(halves)]
+
+    def mine_near(lo, hi):
+        def block(i, carry):
+            n = shares + i
+            mine_load(n).wait()
             rows = pl.ds(pl.multiple_of(i * tile, tile), tile)
-            both = pl.ds(s * halves, halves)
-            arrive(take_ref.at[both, i], o_recv.at[s, i])
-            for h in range(halves):
-                span = slice(h * LANES, (h + 1) * LANES)
-                res_ref[s, span, rows] = (
-                    total[span] + take_ref[s * halves + h, i].astype(jnp.float32)
-                ).astype(res_ref.dtype)
-            pltpu.make_async_copy(
-                res_ref.at[s, :, rows], out_ref.at[s, :, rows], out_sem.at[s]
-            ).start()
+            mine_part_ref[rows] = side_dot(
+                tail_groups, x, lambda j, span: mine_ref[n % 2, :, span] * gate_of(first_mine + i, j)
+            )
+            mine_load(n + 2).start()
             return carry
 
         lax.fori_loop(lo, hi, block, 0)
 
+    def mine_far(lo, hi, late, whole):
+        def block(i, carry):
+            n = 2 * shares - 1 + i
+            if late:
+                late_load(i - 2).wait()
+                source = theirs_ref.at[pl.ds(pl.multiple_of((i - 2) * tile, tile), tile)]
+            else:
+                mine_load(n).wait()
+                source = mine_ref.at[n % 2]
+            rows = pl.ds(pl.multiple_of(i * tile, tile), tile)
+
+            def gated(j, span):
+                return source[:, span] * gate_of(first_mine + i, j)
+
+            total = side_dot(tail_groups, 1 - x, gated)
+            if whole:
+                total += side_dot(tail_groups, x, gated)
+            else:
+                total += mine_part_ref[rows]
+            finish(tail, i, total)
+            return carry
+
+        lax.fori_loop(lo, hi, block, 0)
+
     spread(0)
-    spread(1)
     mask_load.start()
-    for i in range(shares):
-        theirs_load(i).start()
     for n in range(2):
         mine_load(n).start()
     for c in loads[2:]:
         c.wait()
-    for g in range(1, phases // 2):
+    for g in range(1, buffers // 2):
         normalize(g)
-        spread(2 * g)
-        spread(2 * g + 1)
+    for i in range(shares):
+        theirs_load(i).start()
     climb(0)
+    for p in range(1, phases):
+        spread(p)
     make_table()
-    mask_load.wait()
-    gate_theirs()
     relay(0)
     climb(1)
+    mask_load.wait()
+    gate(0, 2)
     sort(0)
     relay(1)
     climb(2)
+    gate(2, 5)
     pass_on(0)
     sort(1)
     relay(2)
@@ -473,11 +533,12 @@
     crossed(1)
     pass_on(2)
     sort(3)
-    theirs(0, 0, 3)
+    theirs(0, 0, 2)
     relay(4)
     climb(5)
-    theirs(0, 3, 5)
+    theirs(0, 2, 4)
     pass_on(3)
+    theirs(0, 4, 5)
     sort(4)
     relay(5)
     climb(6)
@@ -504,20 +565,23 @@
     crossed(4)
     crossed(5)
     pass_on(7)
+    theirs_near([2, 3])
     forward(6, 1)
-    theirs_near([2, 3])
+    mine_near(0, 2)
     forward(7, 0)
-    forward(7, 1)
     forwarded(4)
     forwarded(5)
     theirs_far(2, 0)
+    forward(7, 1)
+    mine_near(2, shares - 1)
     crossed(6)
     crossed(7)
     forwarded(6)
     forwarded(7)
     theirs_far(3, 1)
-    mine(1, 0, 2)
-    mine(1, 2, 5, True)
+    mine_far(0, 2, False, False)
+    mine_far(2, shares - 1, True, False)
+    mine_far(shares - 1, shares, True, True)
     for s in range(snodes):
         pltpu.make_async_copy(res_ref.at[s], out_ref.at[s], out_sem.at[s]).wait()
     arrive(own_ref.at[:, 0:3], b_send)
@@ -525,9 +589,11 @@
         guarded(exists(dz), lambda n=n: arrive(own_ref, c_send.at[n]))
     if depth >= 4:
         guarded(inner, lambda: arrive(own_ref, c_send.at[len(reach)]))
-    arrive(pick_ref, y_send)
+    for k in range(PICKS):
+        arrive(pick_ref.at[k], y_send.at[k])
+    sent = buffers * strip * LANES // tile
     for k in range(2):
-        arrive(pick_ref, x_send.at[k])
+        arrive(theirs_ref.at[0:sent], x_send.at[k])
     arrive(give_ref, o_send)
 
 
@@ -536,35 +602,36 @@
     snodes, tile = diag_inverse.shape[:2]
     held = l_rows.shape[1] // tile
     cfg = sizes(row_size, snodes, tile, held, local_rows, local_cols)
-    phases, blocks, shares, depth = cfg["phases"], cfg["blocks"], cfg["shares"], cfg["depth"]
+    blocks, shares, depth = cfg["blocks"], cfg["shares"], cfg["depth"]
+    phases, buffers = len(cfg["spans"]), cfg["spans"][-1][0] + 1
     strip = tile // PARTS // 2
-    groups = phases // 2
+    groups = buffers // 2
     halves = cfg["halves"]
     away = cfg["away"]
     total = order.shape[1]
     half = shares * tile
     kind = ancestor_inverse.dtype
     dma = pltpu.SemaphoreType.DMA
-    scratch = [pltpu.VMEM((total, strip, LANES), kind) for _ in range(phases)]
-    scratch += [pltpu.VMEM((PARTS, blocks, strip, LANES), kind) for _ in range(phases)]
+    scratch = [pltpu.VMEM((total, size, LANES), kind) for _, _, size in cfg["spans"]]
+    scratch += [pltpu.VMEM((PARTS, blocks, strip, LANES), kind) for _ in range(buffers)]
     scratch += [
         pltpu.VMEM((half, local_cols), kind),
         pltpu.VMEM((2, tile, local_cols), kind),
-        pltpu.VMEM(l_rows.shape, kind),
         pltpu.VMEM(diag_inverse.shape, kind),
         pltpu.VMEM(order.shape, jnp.int32),
         pltpu.VMEM((snodes, total, LANES), jnp.int32),
         pltpu.SMEM((snodes, total, LANES), jnp.int32),
         pltpu.SMEM(mask.shape, jnp.int32),
-        pltpu.VMEM((phases, PARTS, held, strip, LANES), kind),
-        pltpu.VMEM((phases, blocks, strip, LANES), kind),
+        pltpu.VMEM((buffers, PARTS, held, strip, LANES), kind),
+        pltpu.VMEM((PICKS, blocks, strip, LANES), kind),
         pltpu.VMEM((groups, shares, LANES, tile), kind),
         pltpu.VMEM((groups, shares, LANES, tile), kind),
         pltpu.VMEM((snodes, tile, half), kind),
         pltpu.VMEM((half, halves * LANES), jnp.float32),
+        pltpu.VMEM((half, halves * LANES), jnp.float32),
         dma,
         dma((5,)),
-        dma,
+        dma((PICKS,)),
         dma((2,)),
         dma,
         dma((phases,)),
@@ -644,6 +711,7 @@
         and lax.axis_size("row") in (4, 8)
         and tile == 2 * LANES
         and diag_inverse.shape[0] == 2
+        and l_rows.shape[1] * col_size <= ancestor_inverse.shape[0]
         and l_rows.shape[1] % tile == 0
         and ancestor_inverse.shape[0] % (col_size * tile) == 0
     ):

time: 136 us -> 134 us (0.985)
  Pallas kernels: 133 us -> 131 us
    pallas_call x1, Pallas kernels: 133 us -> 131 us  [fused(): pl.pallas_call(functools.partial(fused_kernel, cfg), out_shape=jax.ShapeD...]
where the time goes in v4:
time: 134 us
  Pallas kernels  131 us (98%)
  local copies, waits for them, and re-layouts  2.46 us (2%)
    pallas_call x1, Pallas kernels, fused(): pl.pallas_call(functools.partial(fused_kernel, cfg), out_shape=jax.ShapeD...  131 us

profile of v4, /device:TPU:0, one launch (start us, length us, event | category | flops | bytes accessed | tf_op | source)
XLA Modules:
  0.0 133.8 jit_solution(8555046643295258350)
XLA Ops:
  0.0 131.3 %fused.1 = bf16[2,256,1280]{2,1,0:T(8,128)(2,1)} custom-call(s32[2,80]{1,0:T(2,128)} %order_hbm.1, s32[80,80]{1,0:T(8,128)} %mask_hbm.1, bf16[2560,10240]{1,0:T(8,128)(2,1)} %a_ref.1, bf16[2,1280,256]{2,1,0:T(8,128)(2,1)} %l_ref.1, bf16[2,256,256]{2,1,0:T(8,128)(2,1)} %d_ref.1), custom_call_target="tpu_custom_call" | custom-call | tf_op jit(solution)/shard_map/fused/pallas_call | solution.py:649
  131.3 2.5 %copy.7 = bf16[2,256,1280]{2,1,0:T(8,128)(2,1)} copy(bf16[2,256,1280]{2,1,0:T(8,128)(2,1)} %fused.1) | data formatting | bytes 2621440

commit v5 on v4

--- a/solution.py
+++ b/solution.py
@@ -265,7 +265,7 @@
         sem = f_recv.at[sum(1 for n in range(p) if away[n])]
         return remote(strips(p, lane, span), strips(p, lane, span), x_send.at[k], sem, pair)
 
-    def sort(p):
+    def sort(p, own=True):
         climbed(p)
         if p == 0:
             table_move.wait()
@@ -282,7 +282,8 @@
 
         lax.fori_loop(0, blocks, pick, 0)
         start(lambda: y_copy(p))
-        cross(p, 0)
+        if own:
+            cross(p, 0)
 
     def pass_on(p):
         y_copy(p).wait_recv()
@@ -556,8 +557,9 @@
     forward(4, 0)
     forward(4, 1)
     mine(0, 0, 3)
+    sort(7, False)
     pass_on(6)
-    sort(7)
+    cross(7, 0)
     forward(5, 0)
     forward(5, 1)
     mine(0, 3, 5)

time: 134 us -> 134 us (level)
  no operation moved by 1% of the time
where the time goes in v5:
time: 134 us
  Pallas kernels  131 us (98%)
  local copies, waits for them, and re-layouts  2.46 us (2%)
    pallas_call x1, Pallas kernels, fused(): pl.pallas_call(functools.partial(fused_kernel, cfg), out_shape=jax.ShapeD...  131 us

profile of v5, /device:TPU:0, one launch (start us, length us, event | category | flops | bytes accessed | tf_op | source)
XLA Modules:
  0.0 133.6 jit_solution(4738969057558271963)
XLA Ops:
  0.0 131.1 %fused.1 = bf16[2,256,1280]{2,1,0:T(8,128)(2,1)} custom-call(s32[2,80]{1,0:T(2,128)} %order_hbm.1, s32[80,80]{1,0:T(8,128)} %mask_hbm.1, bf16[2560,10240]{1,0:T(8,128)(2,1)} %a_ref.1, bf16[2,1280,256]{2,1,0:T(8,128)(2,1)} %l_ref.1, bf16[2,256,256]{2,1,0:T(8,128)(2,1)} %d_ref.1), custom_call_target="tpu_custom_call" | custom-call | tf_op jit(solution)/shard_map/fused/pallas_call | solution.py:651
  131.1 2.5 %copy.7 = bf16[2,256,1280]{2,1,0:T(8,128)(2,1)} copy(bf16[2,256,1280]{2,1,0:T(8,128)(2,1)} %fused.1) | data formatting | bytes 2621440
